TPU v7x, 256 devices: a whole 4x4x8 slice. The times are simulated.
256 devices in a mesh: row: 8 (over z), col: 32 (over y, x, core).
Axes of the slice: x: 4, y: 4, z: 8, core: 2. Of those that a mesh axis runs over, the one named last changes fastest.
Arguments:
- sources: float32 [30, 32768], P(None, ('row', 'col')), may hold values from -12 to 12
- log_source_mass: float32 [32768], P(('row', 'col')), may hold values from -4 to 4
- targets: float32 [30, 16384], P(None, 'col'), may hold values from -6 to 6
- log_target_mass: float32 [16384], P('col'), may hold values from -4 to 4
- start_potential: float32 [16384], P('col'), may hold values from -12 to 250
Outputs:
- row_potential: float32 [32768], P(('row', 'col'))
- column_potential: float32 [16384], P('col')
All inputs are finite; a program needn't handle non-finite values.
Results may differ from a plain program's by a relative error of at most 0.00015.
Values sent between devices are 32-bit elements; how exact they have to be, the bound alone decides.
No kernel may reach another device: no remote copies, remote signals or barrier semaphores. Data moves between devices by JAX's collectives and lax.ppermute only.
A program may use at most 64 MiB of HBM per device.

v0:
```python
import math

import jax
import jax.numpy as jnp
from jax import lax
from jax.sharding import PartitionSpec as P

ITERS = 2


entropic_scale = 2.0
lowest = -1e30
block_width = 2048


def merged(shard, axis, combine):
    everything = jax.tree.map(lambda part: lax.all_gather(part, axis), shard)
    leading = jax.tree.map(lambda part: part[0], everything)

    def lap(k, so_far):
        return combine(so_far, jax.tree.map(lambda part: part[k], everything))

    return lax.fori_loop(1, lax.axis_size(axis), lap, leading)


def tile_scores(own_coords, own_sq, other):
    dims = own_coords.shape[0]
    coords = other[:dims]
    inner = lax.dot_general(
        own_coords,
        coords,
        (((0,), (0,)), ((), ())),
        precision=lax.Precision.HIGHEST,
        preferred_element_type=jnp.float32,
    )
    other_sq = 0.5 * jnp.sum(coords * coords, axis=0)
    cost = own_sq[:, None] + other_sq[None, :] - inner
    return other[dims][None, :] - cost / entropic_scale


def merge_pair(first, second):
    peak = jnp.maximum(first[0], second[0])
    return (peak, first[1] * jnp.exp(first[0] - peak) + second[1] * jnp.exp(second[0] - peak))


def online_fold(own_coords, partial_value, piece):
    own_sq = 0.5 * jnp.sum(own_coords * own_coords, axis=0)
    length = piece.shape[1]
    width = math.gcd(length, block_width)
    blocks = piece.reshape(piece.shape[0], length // width, width).transpose(1, 0, 2)

    def advance(running, block):
        scores = tile_scores(own_coords, own_sq, block)
        block_max = jnp.max(scores, axis=1)
        block_sum = jnp.sum(jnp.exp(scores - block_max[:, None]), axis=1)
        return (merge_pair(running, (block_max, block_sum)), None)

    result, unused = lax.scan(advance, partial_value, blocks)
    return result


def column_partials(row_block, all_columns):
    dims = row_block.shape[0] - 1
    coords = all_columns[:dims]
    count = coords.shape[1]
    width = math.gcd(count, block_width)
    blocks = coords.reshape(dims, count // width, width).transpose(1, 0, 2)
    row_sq = 0.5 * jnp.sum(row_block[:dims] * row_block[:dims], axis=0)

    def one_block(block):
        inner = lax.dot_general(
            row_block[:dims],
            block,
            (((0,), (0,)), ((), ())),
            precision=lax.Precision.HIGHEST,
            preferred_element_type=jnp.float32,
        )
        cost = row_sq[:, None] + 0.5 * jnp.sum(block * block, axis=0)[None, :] - inner
        scores = row_block[dims][:, None] - cost / entropic_scale
        block_max = jnp.max(scores, axis=0)
        return (block_max, jnp.sum(jnp.exp(scores - block_max[None, :]), axis=0))

    peaks, totals = lax.map(one_block, blocks)
    return (peaks.reshape(count), totals.reshape(count))


def on_device(sources, log_source_mass, targets, log_target_mass, start_potential):
    own_rows = sources.shape[1]
    own_cols = targets.shape[1]
    target_term = start_potential / entropic_scale + log_target_mass
    row_potential = jnp.zeros((own_rows,), jnp.float32)
    column_potential = start_potential
    for sweep in range(ITERS):
        target_pack = jnp.concatenate([targets, target_term[None, :]], axis=0)
        row_start = (
            jnp.full((own_rows,), lowest, jnp.float32),
            jnp.zeros((own_rows,), jnp.float32),
        )
        gathered = lax.all_gather(target_pack, "col", axis=1, tiled=True)
        row_peak, row_total = online_fold(sources, row_start, gathered)
        row_potential = -entropic_scale * (row_peak + jnp.log(row_total))
        source_term = row_potential / entropic_scale + log_source_mass
        source_pack = jnp.concatenate([sources, source_term[None, :]], axis=0)
        wide_peak, wide_total = column_partials(source_pack, gathered)
        blocks_count = lax.axis_size("col")
        peak_rows, total_rows = (
            lax.all_to_all(
                wide_peak.reshape(blocks_count, own_cols),
                "col",
                split_axis=0,
                concat_axis=0,
                tiled=True,
            ),
            lax.all_to_all(
                wide_total.reshape(blocks_count, own_cols),
                "col",
                split_axis=0,
                concat_axis=0,
                tiled=True,
            ),
        )
        local_peak = jnp.max(peak_rows, axis=0)
        local_total = jnp.sum(total_rows * jnp.exp(peak_rows - local_peak[None, :]), axis=0)
        col_peak, col_total = merged((local_peak, local_total), "row", merge_pair)
        column_potential = -entropic_scale * (col_peak + jnp.log(col_total))
        target_term = column_potential / entropic_scale + log_target_mass
    return (row_potential, column_potential)


def solution(mesh):
    return jax.shard_map(
        on_device,
        mesh=mesh,
        in_specs=(P(None, ("row", "col")), P(("row", "col")), P(None, "col"), P("col"), P("col")),
        out_specs=(P(("row", "col")), P("col")),
        check_vma=False,
    )
```

profile of v0, /device:TPU:2, one launch (start us, length us, event | category | flops | bytes accessed | tf_op | source)
XLA Modules:
  0.0 385.1 jit_solution(970008191891067864)
XLA Ops:
  7.9 1.5 pad_maximum_fusion
  10.2 51.7 %all-gather.11.cloned.1.call-done = f32[31,16384]{1,0:T(8,128)} async-done(((f32[31,512]{1,0:T(8,128)}), f32[31,16384]{1,0:T(8,128)}) %all-gather.11.cloned.1.call-update) | async-done | bytes 2031632 | tf_op jit(solution)/shard_map/all_gather | solution.py:99
  61.8 2.8 copy.31
  64.6 1.4 slice_bitcast_fusion.1
  66.1 42.5 %while.88 = (s32[]{:T(128)}, f32[128]{0:T(128)S(1)}, f32[128]{0:T(128)S(1)}, f32[8,31,2048]{2,0,1:T(8,128)}, f32[128]{0:T(128)S(1)}, /*index=5*/f32[30,128]{1,0:T(8,128)S(1)}, s32[]{:T(128)}, s32[]{:T(128)}, s32[]{}) while((s32[]{:T(128)}, f32[128]{0:T(128)S(1)}, f32[128]{0:T(128)S(1)}, f32[8,31,2048]{2,0,1:T(8,128)}, ...), condition=%wide.region_5.6_spmd.clone, body=%wide.region_1.5_spmd.clone.sunk | while | flops 96330496 | bytes 3158143 | solution.py:58
  66.1 1.9 constant_dynamic-slice_fusion.22
  68.9 2.3 fusion.49
  71.5 1.7 constant_dynamic-slice_fusion.22
  74.2 2.3 fusion.49
  76.8 1.7 constant_dynamic-slice_fusion.22
  79.5 2.3 fusion.49
  82.1 1.7 constant_dynamic-slice_fusion.22
  84.8 2.3 fusion.49
  87.4 1.7 constant_dynamic-slice_fusion.22
  90.1 2.3 fusion.49
  92.7 1.7 constant_dynamic-slice_fusion.22
  95.4 2.3 fusion.49
  98.0 1.7 constant_dynamic-slice_fusion.22
  100.7 2.3 fusion.49
  103.3 1.7 constant_dynamic-slice_fusion.22
  106.0 2.3 fusion.49
  108.6 1.2 copy.32
  110.5 16.6 %while.84 = (s32[]{:T(128)}, f32[8,2048]{1,0:T(8,128)S(1)}, f32[8,2048]{1,0:T(8,128)S(1)}, f32[128]{0:T(128)S(1)}, f32[128]{0:T(128)S(1)}, /*index=5*/f32[8,30,2...) while((s32[]{:T(128)}, f32[8,2048]{1,0:T(8,128)S(1)}, f32[8,2048]{1,0:T(8,128)S(1)}, ...), condition=%wide.region_10.11_spmd, body=%wide.region_6.10_spmd.sunk | while | flops 96325632 | bytes 3186793 | solution.py:83
  115.0 1.2 fusion.45
  117.1 1.2 fusion.45
  119.1 1.2 fusion.45
  121.2 1.2 fusion.45
  123.3 1.2 fusion.45
  125.4 1.2 fusion.45
  127.8 5.8 %all-to-all-start = ((f32[32,1,512]{2,1,0:T(1,128)}), f32[32,1,512]{2,1,0:T(1,128)S(1)}, u32[]{:S(2)}, u32[]{:S(2)}) async-start(f32[32,1,512]{2,1,0:T(1,128)} %all_to_all.32), calls=%async_computation | async-start | bytes 131072 | tf_op jit(solution)/shard_map/all_to_all | solution.py:107
  134.4 5.6 %all-to-all-done = f32[32,1,512]{2,1,0:T(1,128)S(1)} async-done(((f32[32,1,512]{2,1,0:T(1,128)}), f32[32,1,512]{2,1,0:T(1,128)S(1)}, u32[]{:S(2)}, u32[]{:S(2)}) %all-to-all-start) | async-done | bytes 65568 | tf_op jit(solution)/shard_map/all_to_all | solution.py:107
  140.0 4.9 %all-to-all-start.1 = ((f32[32,1,512]{2,1,0:T(1,128)}), f32[32,1,512]{2,1,0:T(1,128)S(1)}, u32[]{:S(2)}, u32[]{:S(2)}) async-start(f32[32,1,512]{2,1,0:T(1,128)} %all_to_all.34), calls=%async_computation.1 | async-start | bytes 131072 | tf_op jit(solution)/shard_map/all_to_all | solution.py:114
  145.0 6.3 %all-to-all-done.1 = f32[32,1,512]{2,1,0:T(1,128)S(1)} async-done(((f32[32,1,512]{2,1,0:T(1,128)}), f32[32,1,512]{2,1,0:T(1,128)S(1)}, u32[]{:S(2)}, u32[]{:S(2)}) %all-to-all-start.1) | async-done | bytes 65568 | tf_op jit(solution)/shard_map/all_to_all | solution.py:114
  151.3 24.1 %all-gather.5 = f32[8,1,512]{2,1,0:T(1,128)S(1)} all-gather(f32[1,1,512]{2,1,0:T(1,128)S(1)} %bitcast.214), channel_id=3, replica_groups=mesh['row'=8,'col'=32] {'row'}, dimensions={0}, use_global_device_ids=true | all-gather | bytes 18432 | tf_op jit(solution)/shard_map/all_gather | solution.py:17
  175.4 21.5 %all-gather.4 = f32[8,1,512]{2,1,0:T(1,128)S(1)} all-gather(f32[1,1,512]{2,1,0:T(1,128)S(1)} %bitcast.213), channel_id=2, replica_groups=mesh['row'=8,'col'=32] {'row'}, dimensions={0}, use_global_device_ids=true | all-gather | bytes 18432 | tf_op jit(solution)/shard_map/all_gather | solution.py:17
  198.0 44.3 %all-gather.13.cloned.1.call-done = f32[31,16384]{1,0:T(8,128)} async-done(((f32[31,512]{1,0:T(8,128)}), f32[31,16384]{1,0:T(8,128)}) %all-gather.13.cloned.1.call-update) | async-done | bytes 2031632 | tf_op jit(solution)/shard_map/all_gather | solution.py:99
  242.3 2.8 copy.33
  245.2 1.4 slice_bitcast_fusion
  246.6 42.5 %while.89 = (s32[]{:T(128)}, f32[128]{0:T(128)S(1)}, f32[128]{0:T(128)S(1)}, f32[8,31,2048]{2,0,1:T(8,128)}, f32[128]{0:T(128)S(1)}, /*index=5*/f32[30,128]{1,0:T(8,128)S(1)}, s32[]{:T(128)}, s32[]{:T(128)}, s32[]{}) while((s32[]{:T(128)}, f32[128]{0:T(128)S(1)}, f32[128]{0:T(128)S(1)}, f32[8,31,2048]{2,0,1:T(8,128)}, ...), condition=%wide.region_19.20_spmd.clone, body=%wide.region_15.0_spmd.clone.sunk | while | flops 96330496 | bytes 3158143 | solution.py:58
  246.6 1.9 constant_dynamic-slice_fusion.24
  249.4 2.3 fusion.52
  252.0 1.7 constant_dynamic-slice_fusion.24
  254.7 2.3 fusion.52
  257.3 1.7 constant_dynamic-slice_fusion.24
  260.0 2.3 fusion.52
  262.6 1.7 constant_dynamic-slice_fusion.24
  265.3 2.3 fusion.52
  267.9 1.7 constant_dynamic-slice_fusion.24
  270.6 2.3 fusion.52
  273.2 1.7 constant_dynamic-slice_fusion.24
  275.9 2.3 fusion.52
  278.5 1.7 constant_dynamic-slice_fusion.24
  281.2 2.3 fusion.52
  283.8 1.7 constant_dynamic-slice_fusion.24
  286.5 2.3 fusion.52
  289.1 1.2 copy.34
  291.1 16.6 %while.86 = (s32[]{:T(128)}, f32[8,2048]{1,0:T(8,128)S(1)}, f32[8,2048]{1,0:T(8,128)S(1)}, f32[128]{0:T(128)S(1)}, f32[128]{0:T(128)S(1)}, /*index=5*/f32[8,30,2...) while((s32[]{:T(128)}, f32[8,2048]{1,0:T(8,128)S(1)}, f32[8,2048]{1,0:T(8,128)S(1)}, ...), condition=%wide.region_24.25_spmd, body=%wide.region_20.24_spmd.sunk | while | flops 96325632 | bytes 3186793 | solution.py:83
  297.6 1.2 fusion.47
  308.4 5.8 %all-to-all-start.2 = ((f32[32,1,512]{2,1,0:T(1,128)}), f32[32,1,512]{2,1,0:T(1,128)S(1)}, u32[]{:S(2)}, u32[]{:S(2)}) async-start(f32[32,1,512]{2,1,0:T(1,128)} %all_to_all.38), calls=%async_computation.2 | async-start | bytes 131072 | tf_op jit(solution)/shard_map/all_to_all | solution.py:107
  314.9 5.6 %all-to-all-done.2 = f32[32,1,512]{2,1,0:T(1,128)S(1)} async-done(((f32[32,1,512]{2,1,0:T(1,128)}), f32[32,1,512]{2,1,0:T(1,128)S(1)}, u32[]{:S(2)}, u32[]{:S(2)}) %all-to-all-start.2) | async-done | bytes 65568 | tf_op jit(solution)/shard_map/all_to_all | solution.py:107
  320.5 4.9 %all-to-all-start.3 = ((f32[32,1,512]{2,1,0:T(1,128)}), f32[32,1,512]{2,1,0:T(1,128)S(1)}, u32[]{:S(2)}, u32[]{:S(2)}) async-start(f32[32,1,512]{2,1,0:T(1,128)} %all_to_all.40), calls=%async_computation.3 | async-start | bytes 131072 | tf_op jit(solution)/shard_map/all_to_all | solution.py:114
  325.5 6.3 %all-to-all-done.3 = f32[32,1,512]{2,1,0:T(1,128)S(1)} async-done(((f32[32,1,512]{2,1,0:T(1,128)}), f32[32,1,512]{2,1,0:T(1,128)S(1)}, u32[]{:S(2)}, u32[]{:S(2)}) %all-to-all-start.3) | async-done | bytes 65568 | tf_op jit(solution)/shard_map/all_to_all | solution.py:114
  331.8 24.1 %all-gather.7 = f32[8,1,512]{2,1,0:T(1,128)S(1)} all-gather(f32[1,1,512]{2,1,0:T(1,128)S(1)} %bitcast.215), channel_id=5, replica_groups=mesh['row'=8,'col'=32] {'row'}, dimensions={0}, use_global_device_ids=true | all-gather | bytes 18432 | tf_op jit(solution)/shard_map/all_gather | solution.py:17
  356.0 21.3 %all-gather.6 = f32[8,1,512]{2,1,0:T(1,128)S(1)} all-gather(f32[1,1,512]{2,1,0:T(1,128)S(1)} %bitcast.212), channel_id=4, replica_groups=mesh['row'=8,'col'=32] {'row'}, dimensions={0}, use_global_device_ids=true | all-gather | bytes 18432 | tf_op jit(solution)/shard_map/all_gather | solution.py:17
  (265 shorter events, 52.6 us)
Async XLA Ops:
  7.2 54.7 %all-gather.11.cloned.1.call-start = ((), (), s32[]{:S(2)}) async-start(), calls=%async_computation.4 | async-start | bytes 2162688 | tf_op jit(solution)/shard_map/all_gather | solution.py:99
  64.6 1.4 copy-start.3
  66.1 42.5 %copy-start = (f32[31,16384]{1,0:T(8,128)S(1)}, f32[31,16384]{1,0:T(8,128)}, u32[]{:S(2)}) copy-start(f32[31,16384]{1,0:T(8,128)} %all-gather.11.cloned.1.call-done) | copy-start | bytes 6094852
  109.8 0.7 copy-start.5
  110.5 86.8 %copy-start.4 = (f32[512]{0:T(512)S(1)}, f32[512]{0:T(512)}, u32[]{:S(2)}) copy-start(f32[512]{0:T(512)} %param.20) | copy-start | bytes 6148
  110.5 86.8 %copy-start.2 = (f32[30,512]{1,0:T(8,128)S(1)}, f32[30,512]{1,0:T(8,128)}, u32[]{:S(2)}) copy-start(f32[30,512]{1,0:T(8,128)} %param.19) | copy-start | bytes 184324
  127.8 12.1 %all-to-all-start = ((f32[32,1,512]{2,1,0:T(1,128)}), f32[32,1,512]{2,1,0:T(1,128)S(1)}, u32[]{:S(2)}, u32[]{:S(2)}) async-start(f32[32,1,512]{2,1,0:T(1,128)} %all_to_all.32), calls=%async_computation | async-start | bytes 131072 | tf_op jit(solution)/shard_map/all_to_all | solution.py:107
  140.0 11.3 %all-to-all-start.1 = ((f32[32,1,512]{2,1,0:T(1,128)}), f32[32,1,512]{2,1,0:T(1,128)S(1)}, u32[]{:S(2)}, u32[]{:S(2)}) async-start(f32[32,1,512]{2,1,0:T(1,128)} %all_to_all.34), calls=%async_computation.1 | async-start | bytes 131072 | tf_op jit(solution)/shard_map/all_to_all | solution.py:114
  144.9 97.5 %all-gather.13.cloned.1.call-start = ((), (), s32[]{:S(2)}) async-start(), calls=%async_computation.5 | async-start | bytes 2162688 | tf_op jit(solution)/shard_map/all_gather | solution.py:99
  246.6 42.5 %copy-start.1 = (f32[31,16384]{1,0:T(8,128)S(1)}, f32[31,16384]{1,0:T(8,128)}, u32[]{:S(2)}) copy-start(f32[31,16384]{1,0:T(8,128)} %all-gather.13.cloned.1.call-done) | copy-start | bytes 6094852
  308.4 12.1 %all-to-all-start.2 = ((f32[32,1,512]{2,1,0:T(1,128)}), f32[32,1,512]{2,1,0:T(1,128)S(1)}, u32[]{:S(2)}, u32[]{:S(2)}) async-start(f32[32,1,512]{2,1,0:T(1,128)} %all_to_all.38), calls=%async_computation.2 | async-start | bytes 131072 | tf_op jit(solution)/shard_map/all_to_all | solution.py:107
  320.5 11.3 %all-to-all-start.3 = ((f32[32,1,512]{2,1,0:T(1,128)}), f32[32,1,512]{2,1,0:T(1,128)S(1)}, u32[]{:S(2)}, u32[]{:S(2)}) async-start(f32[32,1,512]{2,1,0:T(1,128)} %all_to_all.40), calls=%async_computation.3 | async-start | bytes 131072 | tf_op jit(solution)/shard_map/all_to_all | solution.py:114
Sparse Core Ops, SparseCore 0:
  10.6 51.2 all-gather.10
  198.1 44.1 all-gather.12
where the time goes:
time: 387 us; the launch traced here: 385 us
  waiting for transfers between devices  120 us (31%)
  blocking collectives  91 us (24%)
  local copies, waits for them, and re-layouts  65.8 us (17%)
  matrix products  54.9 us (14%)
  starting transfers between devices  21.6 us (6%)
  other arithmetic  15.7 us (4%)
  between operations  14.3 us (4%)
    all_gather x2, waiting for transfers between devices, on_device(): gathered = lax.all_gather(target_pack, 'col', axis=1, tiled=True)  96 us
    all_gather x4, blocking collectives, merged(): everything = jax.tree.map(lambda part: lax.all_gather(part, axis), shard)  91 us
    dot_general x16, matrix products, tile_scores(): lax.dot_general(own_coords, coords, (((0,), (0,)), ((), ())), precision=l...  36.3 us
    slice x16, local copies, waits for them, and re-layouts, tile_scores(): coords = other[:dims]  28 us
    dot_general x16, matrix products, one_block(): lax.dot_general(row_block[:dims], block, (((0,), (0,)), ((), ())), precis...  18.6 us
    slice x16, local copies, waits for them, and re-layouts, tile_scores(): return other[dims][None, :] - cost / entropic_scale  13.7 us
    all_to_all x2, waiting for transfers between devices, on_device(): lax.all_to_all(wide_total.reshape(blocks_count, own_cols), 'col', split_a...  12.6 us
    all_to_all x2, starting transfers between devices, on_device(): lax.all_to_all(wide_peak.reshape(blocks_count, own_cols), 'col', split_ax...  11.7 us
  transfers between devices with their start and end apart: 6, of which 6 were waited for; matrix products, arithmetic and copies ran while one was open for 0% of the time, Pallas kernels for 0%

commit v1 on v0

v1 whole, which is shorter than its diff:
```python
import functools
import math

import jax
import jax.numpy as jnp
from jax import lax
from jax.experimental import pallas as pl
from jax.experimental.pallas import tpu as pltpu
from jax.sharding import Mesh, PartitionSpec as P

LOG2E = math.log2(math.e)
LN2 = math.log(2.0)
LANES = 128
ROWS = 32
LEFT = (0, 0, 1, 1, 0, 2)
RIGHT = (0, 1, 0, 1, 2, 0)
LOWEST = -1e30
F32, BF16 = jnp.float32, jnp.bfloat16


def parts_of(value):
    first = value.astype(BF16)
    rest = value - first.astype(F32)
    second = rest.astype(BF16)
    third = (rest - second.astype(F32)).astype(BF16)
    return first, second, third


def merge(values):
    peak = jnp.max(values, axis=0)
    return peak + LOG2E * jnp.log(jnp.sum(jnp.exp2(values - peak[None]), axis=0))


def row_of(shape, row):
    return lax.broadcasted_iota(jnp.int32, shape, 0) == row


def with_row(block, row, value):
    return jnp.where(row_of(block.shape, row), value, block)


def fold(left_ref, right_ref, step):
    count, width = left_ref.shape[1], right_ref.shape[1]
    peak = jnp.full((8, width), LOWEST, F32)
    total = jnp.zeros((8, width), F32)
    for at in range(0, count, step):
        scores = lax.dot_general(
            left_ref[:, at : at + step],
            right_ref[...],
            (((0,), (0,)), ((), ())),
            preferred_element_type=F32,
        ).reshape(step // 8, 8, width)
        new_peak = jnp.maximum(peak, jnp.max(scores, axis=0))
        total = total * jnp.exp2(peak - new_peak) + jnp.sum(jnp.exp2(scores - new_peak[None]), axis=0)
        peak = new_peak
    top = jnp.max(peak, axis=0, keepdims=True)
    whole = jnp.sum(total * jnp.exp2(peak - top), axis=0, keepdims=True)
    return top + LOG2E * jnp.log(whole)


def as_rows(line):
    return [line[:, at : at + LANES] for at in range(0, line.shape[1], LANES)]


def send_to_all(line, out_ref):
    for at, piece in enumerate(as_rows(line)):
        out_ref[:, at, :] = jnp.broadcast_to(piece, (out_ref.shape[0], LANES))


def pack_kernel(src_ref, src_mass_ref, tgt_ref, tgt_mass_ref, start_ref, src_out, tgt_out):
    dims = src_ref.shape[0]
    block = jnp.concatenate([src_ref[...], src_mass_ref[...], jnp.zeros((1, LANES), F32)], axis=0)
    src_out[...] = jnp.broadcast_to(block[None], src_out.shape)
    tgt_out[...] = jnp.concatenate([tgt_ref[...], tgt_mass_ref[...], start_ref[...]], axis=0)


def set_beta(tgt_ref, at, beta):
    lanes = slice(at, at + beta.shape[1])
    for slot, part in enumerate(parts_of(beta)):
        rows = slice(slot * ROWS, slot * ROWS + ROWS)
        block = tgt_ref[rows, lanes].astype(F32)
        tgt_ref[rows, lanes] = with_row(block, ROWS - 2, part.astype(F32)).astype(BF16)


def first_kernel(dims, y_count, src_ref, *refs):
    tgt_refs = refs[:y_count]
    row_out, src_out, tgt_out, src_mass_out, tgt_mass_out = refs[y_count : y_count + 5]
    held = refs[y_count + 5]
    y = lax.axis_index("y")
    for shift in range(y_count):
        held[lax.rem(y + y_count - shift, y_count)] = tgt_refs[shift][...]
    groups = src_ref.shape[0]
    for group in range(groups):
        block = src_ref[group]
        src_mass_out[group : group + 1, :] = LOG2E * block[dims : dims + 1, :]
        spare = lax.broadcasted_iota(jnp.int32, block.shape, 0) >= dims
        split = parts_of(jnp.where(spare, 0.0, (0.5 * LOG2E) * block))
        lanes = slice(group * LANES, group * LANES + LANES)
        for slot, which in enumerate(LEFT):
            piece = split[which].astype(F32)
            if slot < 3:
                piece = with_row(piece, ROWS - 2, 1.0)
            src_out[slot * ROWS : slot * ROWS + ROWS, lanes] = piece.astype(BF16)
    width = held.shape[2]
    for group in range(y_count):
        block = held[group]
        mass = LOG2E * block[dims : dims + 1, :]
        for at, piece in enumerate(as_rows(mass)):
            row = group * (width // LANES) + at
            tgt_mass_out[row : row + 1, :] = piece
        spare = lax.broadcasted_iota(jnp.int32, block.shape, 0) >= dims
        coords = jnp.where(spare, 0.0, block)
        split = parts_of(coords)
        norm = jnp.sum(coords * coords, axis=0, keepdims=True)
        beta = mass + LOG2E * (0.5 * block[dims + 1 : dims + 2, :] - 0.25 * norm)
        beta_parts = parts_of(beta)
        lanes = slice(group * width, group * width + width)
        for slot, which in enumerate(RIGHT):
            piece = split[which].astype(F32)
            if slot < 3:
                piece = with_row(piece, ROWS - 2, beta_parts[slot].astype(F32))
                piece = with_row(piece, ROWS - 1, 1.0)
            tgt_out[slot * ROWS : slot * ROWS + ROWS, lanes] = piece.astype(BF16)
    send_to_all(fold(tgt_out, src_out, 512), row_out)


def column_line(rows_ref, src_ref, src_mass_ref, tgt_ref, own_src, step):
    merged = merge(rows_ref[...])
    alpha = src_mass_ref[...] - merged
    split = parts_of(alpha)
    own_src[...] = src_ref[...]
    for group in range(alpha.shape[0]):
        lanes = slice(group * LANES, group * LANES + LANES)
        for slot in range(3):
            rows = slice(slot * ROWS, slot * ROWS + ROWS)
            block = with_row(src_ref[rows, lanes].astype(F32), ROWS - 2, 0.0)
            value = split[slot][group : group + 1, :].astype(F32)
            own_src[rows, lanes] = with_row(block, ROWS - 1, value).astype(BF16)
    return merged, fold(own_src, tgt_ref, step)


def column_kernel(rows_ref, src_ref, src_mass_ref, tgt_ref, col_out, own_src):
    unused, line = column_line(rows_ref, src_ref, src_mass_ref, tgt_ref, own_src, 256)
    send_to_all(line, col_out)


def row_kernel(cols_ref, src_ref, tgt_ref, tgt_mass_ref, row_out, own_tgt):
    beta = tgt_mass_ref[...] - merge(cols_ref[...])
    own_tgt[...] = tgt_ref[...]
    for group in range(beta.shape[0]):
        set_beta(own_tgt, group * LANES, beta[group : group + 1, :])
    send_to_all(fold(own_tgt, src_ref, 512), row_out)


def last_column_kernel(
    x_axes, y_count, rows_ref, src_ref, src_mass_ref, tgt_ref, own_ref, col_out, pot_out, own_src, kept
):
    merged, line = column_line(rows_ref, src_ref, src_mass_ref, tgt_ref, own_src, 256)
    kept[...] = merged
    mine = kept[pl.ds(lax.axis_index(x_axes), 1), :]
    coords = own_ref[...]
    norm = jnp.sum(coords * coords, axis=0, keepdims=True)
    pot_out[...] = 0.5 * norm - (2.0 * LN2) * mine
    pieces = as_rows(line)
    share = len(pieces) // y_count
    for to in range(col_out.shape[0]):
        for at in range(share):
            col_out[to, at : at + 1, :] = pieces[(to % y_count) * share + at]


def final_kernel(cols_ref, tgt_ref, pot_out):
    merged = merge(cols_ref[...])
    coords = tgt_ref[...]
    norm = jnp.sum(coords * coords, axis=0, keepdims=True)
    for at, piece in enumerate(as_rows(norm)):
        pot_out[at : at + 1, :] = 0.5 * piece - (2.0 * LN2) * merged[at : at + 1, :]


def call(kernel, outs, scratch=()):
    return pl.pallas_call(
        kernel,
        out_shape=outs,
        scratch_shapes=list(scratch),
        compiler_params=pltpu.CompilerParams(vmem_limit_bytes=24 * 1024 * 1024),
    )


def shape(*dims, dtype=F32):
    return jax.ShapeDtypeStruct(dims, dtype)


def on_device(sources, log_source_mass, targets, log_target_mass, start_potential):
    near, far = ("x", "c"), ("z", "y")
    dims, own_rows = sources.shape
    own_cols = targets.shape[1]
    near_count, y_count = lax.axis_size(near), lax.axis_size("y")
    far_count = lax.axis_size(far)
    rows, cols = near_count * own_rows, y_count * own_cols
    row_tiles, col_tiles = rows // LANES, cols // LANES
    depth = len(LEFT) * ROWS

    def swap(value, axes):
        return lax.all_to_all(value, axes, 0, 0, tiled=True)

    src_send, tgt_own = call(pack_kernel, (shape(near_count, ROWS, LANES), shape(ROWS, own_cols)))(
        sources, log_source_mass[None], targets, log_target_mass[None], start_potential[None]
    )
    tgts = [tgt_own] + [
        lax.ppermute(tgt_own, "y", [(k, (k + shift) % y_count) for k in range(y_count)])
        for shift in range(1, y_count)
    ]
    src_all = swap(src_send, near)
    row_send, src, tgt, src_mass, tgt_mass = call(
        functools.partial(first_kernel, dims, y_count),
        (
            shape(near_count, row_tiles, LANES),
            shape(depth, rows, dtype=BF16),
            shape(depth, cols, dtype=BF16),
            shape(row_tiles, LANES),
            shape(col_tiles, LANES),
        ),
        [pltpu.VMEM((y_count, ROWS, own_cols), F32)],
    )(src_all, *tgts)
    row_all = swap(row_send, near)
    col_send = call(
        column_kernel, shape(far_count, col_tiles, LANES), [pltpu.VMEM((depth, rows), BF16)]
    )(row_all, src, src_mass, tgt)
    col_all = swap(col_send, far)
    row_send = call(
        row_kernel, shape(near_count, row_tiles, LANES), [pltpu.VMEM((depth, cols), BF16)]
    )(col_all, src, tgt, tgt_mass)
    row_all = swap(row_send, near)
    col_send, row_potential = call(
        functools.partial(last_column_kernel, near, y_count),
        (shape(far_count, own_cols // LANES, LANES), shape(1, own_rows)),
        [pltpu.VMEM((depth, rows), BF16), pltpu.VMEM((row_tiles, LANES), F32)],
    )(row_all, src, src_mass, tgt, sources)
    col_all = swap(col_send, far)
    column_potential = call(final_kernel, shape(own_cols // LANES, LANES))(col_all, targets)
    return row_potential.reshape(own_rows), column_potential.reshape(own_cols)


def solution(mesh):
    split = Mesh(mesh.devices.reshape(8, 4, 4, 2), ("z", "y", "x", "c"))
    everywhere, column = ("z", "y", "x", "c"), ("y", "x", "c")
    return jax.shard_map(
        on_device,
        mesh=split,
        in_specs=(P(None, everywhere), P(everywhere), P(None, column), P(column), P(column)),
        out_specs=(P(everywhere), P(column)),
        check_vma=False,
    )
```

time: 387 us -> 81.5 us (0.21)
  waiting for transfers between devices: 120 us -> 5.14 us
  local copies, waits for them, and re-layouts: 65.8 us -> 2.24 us
  matrix products: 54.9 us -> 0 us
  blocking collectives: 91 us -> 52.3 us
  other arithmetic: 15.7 us -> 0 us
  between operations: 14.3 us -> 0.68 us
  starting transfers between devices: 21.6 us -> 9.45 us
  Pallas kernels: 0 us -> 10.9 us
    all_gather x2 -> x0, waiting for transfers between devices: 96 us -> none  [on_device(): gathered = lax.all_gather(target_pack, 'col', axis=1, tiled=True)]
    all_gather x4 -> x0, blocking collectives: 91 us -> none  [merged(): everything = jax.tree.map(lambda part: lax.all_gather(part, axis), shard)]
    dot_general x32 -> x0, matrix products: 54.9 us -> none  [the longest x16 36.3 us: tile_scores(): lax.dot_general(own_coords, coords, (((0,), (0,)), ((), ())), precision=l...]
    all_to_all x0 -> x4, blocking collectives: none -> 52.3 us  [swap(): return lax.all_to_all(value, axes, 0, 0, tiled=True)]
    slice x36 -> x0, local copies, waits for them, and re-layouts: 41.7 us -> none  [the longest x16 28 us: tile_scores(): coords = other[:dims]]
    all_to_all x4 -> x1, waiting for transfers between devices: 23.8 us -> 0.01 us  [swap(): return lax.all_to_all(value, axes, 0, 0, tiled=True)]
    all_to_all x4 -> x1, starting transfers between devices: 21.5 us -> 5.52 us  [swap(): return lax.all_to_all(value, axes, 0, 0, tiled=True)]
    pallas_call x0 -> x6, Pallas kernels: none -> 10.9 us  [the longest x1 2.56 us: on_device(): call(functools.partial(last_column_kernel, near, y_count), (shape(far_cou...]
  transfers between devices with their start and end apart: 6 -> 4, of which waited for: 6 -> 3; matrix products, arithmetic and copies ran while one was open for 0% -> 0% of each run, Pallas kernels for 0% -> 0%
where the time goes in v1:
time: 81.5 us; the launch traced here: 80.8 us
  blocking collectives  52.3 us (64%)
  Pallas kernels  10.9 us (13%)
  starting transfers between devices  9.45 us (12%)
  waiting for transfers between devices  5.14 us (6%)
  local copies, waits for them, and re-layouts  2.24 us (3%)
    all_to_all x4, blocking collectives, swap(): return lax.all_to_all(value, axes, 0, 0, tiled=True)  52.3 us
    all_to_all x1, starting transfers between devices, swap(): return lax.all_to_all(value, axes, 0, 0, tiled=True)  5.52 us
    ppermute x3, waiting for transfers between devices, on_device(): lax.ppermute(tgt_own, 'y', [(k, (k + shift) % y_count) for k in range(y_c...  5.14 us
    ppermute x3, starting transfers between devices, on_device(): lax.ppermute(tgt_own, 'y', [(k, (k + shift) % y_count) for k in range(y_c...  3.93 us
    pallas_call x1, Pallas kernels, on_device(): call(functools.partial(last_column_kernel, near, y_count), (shape(far_cou...  2.56 us
    pallas_call x1, Pallas kernels, on_device(): call(row_kernel, shape(near_count, row_tiles, LANES), [pltpu.VMEM((depth,...  2.43 us
    pallas_call x1, Pallas kernels, on_device(): call(functools.partial(first_kernel, dims, y_count), (shape(near_count, r...  2.41 us
    pallas_call x1, Pallas kernels, on_device(): call(column_kernel, shape(far_count, col_tiles, LANES), [pltpu.VMEM((dept...  2.25 us
  transfers between devices with their start and end apart: 4, of which 3 were waited for; matrix products, arithmetic and copies ran while one was open for 0% of the time, Pallas kernels for 0%

profile of v1, /device:TPU:2, one launch (start us, length us, event | category | flops | bytes accessed | tf_op | source)
XLA Modules:
  0.0 80.8 jit_solution(15840725063256196020)
XLA Ops:
  0.6 0.0 copy-start.5
  0.6 0.0 copy-start.4
  0.7 0.0 copy-start.6
  0.7 0.7 copy-done.5
  1.3 0.0 copy-done.4
  1.3 0.0 copy-done.6
  1.3 0.0 copy-start
  1.3 0.8 %copy-done = f32[30,512]{1,0:T(8,128)S(1)} copy-done((f32[30,512]{1,0:T(8,128)S(1)}, f32[30,512]{1,0:T(8,128)}, u32[]{:S(2)}) %copy-start) | copy-done | bytes 61464
  2.2 0.0 copy-start.2
  2.2 0.7 copy-done.2
  2.9 0.7 shard_map.68
  3.6 5.5 %all-to-all-start = ((f32[8,32,128]{2,1,0:T(8,128)}), f32[8,32,128]{2,1,0:T(8,128)S(1)}, u32[]{:S(2)}, u32[]{:S(2)}) async-start(f32[8,32,128]{2,1,0:T(8,128)} %get-tuple-element.11), calls=%async_computation | async-start | bytes 262144 | tf_op jit(solution)/shard_map/all_to_all | solution.py:203
  9.1 2.3 %collective-permute-start.2 = (f32[32,512]{1,0:T(8,128)S(1)}, f32[32,512]{1,0:T(8,128)S(1)}, u32[]{:S(2)}, u32[]{:S(2)}) collective-permute-start(f32[32,512]{1,0:T(8,128)S(1)} %get-tuple-element.12.refs_0_), channel_id=1, source_target_pairs={{0,24},{8,0},{16,8},{24,16},{1,25},{9,1},{17,9},{25,17},{2,26},{10... | collective-permute-start | bytes 196616 | tf_op jit(solution)/shard_map/ppermute | solution.py:209
  11.4 0.6 collective-permute-start.1
  12.0 1.0 %collective-permute-start = (f32[32,512]{1,0:T(8,128)S(1)}, f32[32,512]{1,0:T(8,128)S(1)}, u32[]{:S(2)}, u32[]{:S(2)}) collective-permute-start(f32[32,512]{1,0:T(8,128)S(1)} %get-tuple-element.12.refs_0_), channel_id=1, source_target_pairs={{0,8},{8,16},{16,24},{24,0},{1,9},{9,17},{17,25},{25,1},{2,10},{10... | collective-permute-start | bytes 196616 | tf_op jit(solution)/shard_map/ppermute | solution.py:209
  13.0 1.5 %collective-permute-done.2.refs_3_ = f32[32,512]{1,0:T(8,128)S(1)} collective-permute-done((f32[32,512]{1,0:T(8,128)S(1)}, f32[32,512]{1,0:T(8,128)S(1)}, u32[]{:S(2)}, u32[]{:S(2)}) %collective-permute-start.2) | collective-permute-done | bytes 65568 | tf_op jit(solution)/shard_map/ppermute | solution.py:209
  14.5 2.9 %collective-permute-done.1.refs_2_ = f32[32,512]{1,0:T(8,128)S(1)} collective-permute-done((f32[32,512]{1,0:T(8,128)S(1)}, f32[32,512]{1,0:T(8,128)S(1)}, u32[]{:S(2)}, u32[]{:S(2)}) %collective-permute-start.1) | collective-permute-done | bytes 65568 | tf_op jit(solution)/shard_map/ppermute | solution.py:209
  17.4 0.7 collective-permute-done.refs_1_
  18.1 0.0 all-to-all-done.src_ref
  18.1 2.4 %shard_map.69 = (f32[8,8,128]{2,1,0:T(8,128)S(1)}, bf16[192,1024]{1,0:T(8,128)(2,1)S(1)}, bf16[192,2048]{1,0:T(8,128)(2,1)S(1)}, f32[8,128]{1,0:T(8,128)S(1)}, f32[16,128]{1,0:T(8,128)S(1)}) custom-call(f32[8,32,128]{2,1,0:T(8,128)S(1)} %all-to-all-done.src_ref, f32[32,512]{1,0:T(8,128)S(1)} %get-tuple-element.12.refs_0_, ...), custom_call_target="tpu_custom_call" | custom-call | tf_op jit(solution)/shard_map/pallas_call | solution.py:213
  20.6 8.6 %all_to_all.25.rows_ref = f32[8,8,128]{2,1,0:T(8,128)S(1)} all-to-all(f32[8,8,128]{2,1,0:T(8,128)S(1)} %get-tuple-element.13), channel_id=1, replica_groups=mesh['z'=8,'y'=4,'x'=4,'c'=2] {'x','c'}, dimensions={0} | all-to-all | bytes 65536 | tf_op jit(solution)/shard_map/all_to_all | solution.py:203
  29.1 2.3 %shard_map.70 = f32[32,16,128]{2,1,0:T(8,128)S(1)} custom-call(f32[8,8,128]{2,1,0:T(8,128)S(1)} %all_to_all.25.rows_ref, bf16[192,1024]{1,0:T(8,128)(2,1)S(1)} %get-tuple-element.14.src_ref, f32[8,128]{1,0:T(8,128)S(1)} %get-tuple-element.15.src_mass_ref, bf16[192,2048]{1,0:T(8,128)(2,1)S(1)} %get-tuple-element.16.tgt_ref), custom_call_target="tpu_custom_call" | custom-call | tf_op jit(solution)/shard_map/pallas_call | solution.py:225
  31.4 21.8 %all_to_all.26.cols_ref = f32[32,16,128]{2,1,0:T(8,128)S(1)} all-to-all(f32[32,16,128]{2,1,0:T(8,128)S(1)} %shard_map.70), channel_id=1, replica_groups=mesh['z'=8,'y'=4,'x'=4,'c'=2] {'z','y'}, dimensions={0} | all-to-all | bytes 524288 | tf_op jit(solution)/shard_map/all_to_all | solution.py:203
  53.2 2.4 %shard_map.71 = f32[8,8,128]{2,1,0:T(8,128)S(1)} custom-call(f32[32,16,128]{2,1,0:T(8,128)S(1)} %all_to_all.26.cols_ref, bf16[192,1024]{1,0:T(8,128)(2,1)S(1)} %get-tuple-element.14.src_ref, bf16[192,2048]{1,0:T(8,128)(2,1)S(1)} %get-tuple-element.16.tgt_ref, f32[16,128]{1,0:T(8,128)S(1)} %get-tuple-element.17.tgt_mass_ref), custom_call_target="tpu_custom_call" | custom-call | tf_op jit(solution)/shard_map/pallas_call | solution.py:229
  55.6 0.0 copy-start.3
  55.6 8.0 %all_to_all.27.rows_ref = f32[8,8,128]{2,1,0:T(8,128)S(1)} all-to-all(f32[8,8,128]{2,1,0:T(8,128)S(1)} %shard_map.71), channel_id=1, replica_groups=mesh['z'=8,'y'=4,'x'=4,'c'=2] {'x','c'}, dimensions={0} | all-to-all | bytes 65536 | tf_op jit(solution)/shard_map/all_to_all | solution.py:203
  63.6 0.0 copy-done.3
  63.6 2.6 %shard_map.72 = (f32[32,4,128]{2,1,0:T(4,128)S(1)}, f32[1,128]{1,0:T(1,128)}) custom-call(f32[8,8,128]{2,1,0:T(8,128)S(1)} %all_to_all.27.rows_ref, bf16[192,1024]{1,0:T(8,128)(2,1)S(1)} %get-tuple-element.14.src_ref, f32[8,128]{1,0:T(8,128)S(1)} %get-tuple-element.15.src_mass_ref, bf16[192,2048]{1,0:T(8,128)(2,1)S(1)} %get-tuple-element.16.tgt_ref, ...), custom_call_target="tpu_custom_call" | custom-call | tf_op jit(solution)/shard_map/pallas_call | solution.py:233
  66.1 0.0 copy-start.1
  66.1 14.0 %all_to_all.28.cols_ref = f32[32,4,128]{2,1,0:T(4,128)S(1)} all-to-all(f32[32,4,128]{2,1,0:T(4,128)S(1)} %get-tuple-element.19), channel_id=1, replica_groups=mesh['z'=8,'y'=4,'x'=4,'c'=2] {'z','y'}, dimensions={0} | all-to-all | bytes 131072 | tf_op jit(solution)/shard_map/all_to_all | solution.py:203
  80.1 0.0 copy-done.1
  80.1 0.6 shard_map.73
Async XLA Ops:
  0.6 0.7 copy-start.5
  0.6 0.7 copy-start.4
  0.7 0.7 copy-start.6
  1.3 0.8 %copy-start = (f32[30,512]{1,0:T(8,128)S(1)}, f32[30,512]{1,0:T(8,128)}, u32[]{:S(2)}) copy-start(f32[30,512]{1,0:T(8,128)} %tgt_ref.3) | copy-start | bytes 184324
  2.2 0.7 copy-start.2
  3.6 14.6 %all-to-all-start = ((f32[8,32,128]{2,1,0:T(8,128)}), f32[8,32,128]{2,1,0:T(8,128)S(1)}, u32[]{:S(2)}, u32[]{:S(2)}) async-start(f32[8,32,128]{2,1,0:T(8,128)} %get-tuple-element.11), calls=%async_computation | async-start | bytes 262144 | tf_op jit(solution)/shard_map/all_to_all | solution.py:203
  9.1 5.5 %collective-permute-start.2 = (f32[32,512]{1,0:T(8,128)S(1)}, f32[32,512]{1,0:T(8,128)S(1)}, u32[]{:S(2)}, u32[]{:S(2)}) collective-permute-start(f32[32,512]{1,0:T(8,128)S(1)} %get-tuple-element.12.refs_0_), channel_id=1, source_target_pairs={{0,24},{8,0},{16,8},{24,16},{1,25},{9,1},{17,9},{25,17},{2,26},{10... | collective-permute-start | bytes 196616 | tf_op jit(solution)/shard_map/ppermute | solution.py:209
  11.4 6.0 %collective-permute-start.1 = (f32[32,512]{1,0:T(8,128)S(1)}, f32[32,512]{1,0:T(8,128)S(1)}, u32[]{:S(2)}, u32[]{:S(2)}) collective-permute-start(f32[32,512]{1,0:T(8,128)S(1)} %get-tuple-element.12.refs_0_), channel_id=1, source_target_pairs={{0,16},{8,24},{16,0},{24,8},{1,17},{9,25},{17,1},{25,9},{2,18},{10... | collective-permute-start | bytes 196616 | tf_op jit(solution)/shard_map/ppermute | solution.py:209
  12.0 6.1 %collective-permute-start = (f32[32,512]{1,0:T(8,128)S(1)}, f32[32,512]{1,0:T(8,128)S(1)}, u32[]{:S(2)}, u32[]{:S(2)}) collective-permute-start(f32[32,512]{1,0:T(8,128)S(1)} %get-tuple-element.12.refs_0_), channel_id=1, source_target_pairs={{0,8},{8,16},{16,24},{24,0},{1,9},{9,17},{17,25},{25,1},{2,10},{10... | collective-permute-start | bytes 196616 | tf_op jit(solution)/shard_map/ppermute | solution.py:209
  55.6 8.0 %copy-start.3 = (f32[30,128]{1,0:T(8,128)S(1)}, f32[30,128]{1,0:T(8,128)}, u32[]{:S(2)}) copy-start(f32[30,128]{1,0:T(8,128)} %own_ref.1) | copy-start | bytes 46084
  66.1 14.0 %copy-start.1 = (f32[30,512]{1,0:T(8,128)S(1)}, f32[30,512]{1,0:T(8,128)}, u32[]{:S(2)}) copy-start(f32[30,512]{1,0:T(8,128)} %tgt_ref.3) | copy-start | bytes 184324

commit v2 on v1

--- a/solution.py
+++ b/solution.py
@@ -7,6 +7,7 @@
 from jax.experimental import pallas as pl
 from jax.experimental.pallas import tpu as pltpu
 from jax.sharding import Mesh, PartitionSpec as P
+
 
 LOG2E = math.log2(math.e)
 LN2 = math.log(2.0)
@@ -67,11 +68,20 @@
         out_ref[:, at, :] = jnp.broadcast_to(piece, (out_ref.shape[0], LANES))
 
 
-def pack_kernel(src_ref, src_mass_ref, tgt_ref, tgt_mass_ref, start_ref, src_out, tgt_out):
-    dims = src_ref.shape[0]
-    block = jnp.concatenate([src_ref[...], src_mass_ref[...], jnp.zeros((1, LANES), F32)], axis=0)
+def pack_kernel(*refs):
+    inputs, (src_out, tgt_out), held, sems = refs[:5], refs[5:7], refs[7:12], refs[12]
+    copies = [
+        pltpu.make_async_copy(whence, where, sems.at[at])
+        for at, (whence, where) in enumerate(zip(inputs, held))
+    ]
+    for copy in copies:
+        copy.start()
+    for copy in copies:
+        copy.wait()
+    src, src_mass, tgt, tgt_mass, start = (ref[...] for ref in held)
+    tgt_out[...] = jnp.concatenate([tgt, tgt_mass, start], axis=0)
+    block = jnp.concatenate([src, src_mass, jnp.zeros((1, LANES), F32)], axis=0)
     src_out[...] = jnp.broadcast_to(block[None], src_out.shape)
-    tgt_out[...] = jnp.concatenate([tgt_ref[...], tgt_mass_ref[...], start_ref[...]], axis=0)
 
 
 def set_beta(tgt_ref, at, beta):
@@ -82,13 +92,13 @@
         tgt_ref[rows, lanes] = with_row(block, ROWS - 2, part.astype(F32)).astype(BF16)
 
 
-def first_kernel(dims, y_count, src_ref, *refs):
-    tgt_refs = refs[:y_count]
-    row_out, src_out, tgt_out, src_mass_out, tgt_mass_out = refs[y_count : y_count + 5]
-    held = refs[y_count + 5]
-    y = lax.axis_index("y")
-    for shift in range(y_count):
-        held[lax.rem(y + y_count - shift, y_count)] = tgt_refs[shift][...]
+def first_kernel(dims, share_count, src_ref, *refs):
+    tgt_refs = refs[:share_count]
+    row_out, src_out, tgt_out, src_mass_out, tgt_mass_out = refs[share_count : share_count + 5]
+    held = refs[share_count + 5]
+    mine = lax.axis_index("c")
+    for shift in range(share_count):
+        held[lax.rem(mine + share_count - shift, share_count)] = tgt_refs[shift][...]
     groups = src_ref.shape[0]
     for group in range(groups):
         block = src_ref[group]
@@ -102,7 +112,7 @@
                 piece = with_row(piece, ROWS - 2, 1.0)
             src_out[slot * ROWS : slot * ROWS + ROWS, lanes] = piece.astype(BF16)
     width = held.shape[2]
-    for group in range(y_count):
+    for group in range(share_count):
         block = held[group]
         mass = LOG2E * block[dims : dims + 1, :]
         for at, piece in enumerate(as_rows(mass)):
@@ -121,7 +131,7 @@
                 piece = with_row(piece, ROWS - 2, beta_parts[slot].astype(F32))
                 piece = with_row(piece, ROWS - 1, 1.0)
             tgt_out[slot * ROWS : slot * ROWS + ROWS, lanes] = piece.astype(BF16)
-    send_to_all(fold(tgt_out, src_out, 512), row_out)
+    send_to_all(fold(tgt_out, src_out, 256), row_out)
 
 
 def column_line(rows_ref, src_ref, src_mass_ref, tgt_ref, own_src, step):
@@ -140,7 +150,7 @@
 
 
 def column_kernel(rows_ref, src_ref, src_mass_ref, tgt_ref, col_out, own_src):
-    unused, line = column_line(rows_ref, src_ref, src_mass_ref, tgt_ref, own_src, 256)
+    _, line = column_line(rows_ref, src_ref, src_mass_ref, tgt_ref, own_src, 512)
     send_to_all(line, col_out)
 
 
@@ -149,23 +159,23 @@
     own_tgt[...] = tgt_ref[...]
     for group in range(beta.shape[0]):
         set_beta(own_tgt, group * LANES, beta[group : group + 1, :])
-    send_to_all(fold(own_tgt, src_ref, 512), row_out)
+    send_to_all(fold(own_tgt, src_ref, 256), row_out)
 
 
 def last_column_kernel(
-    x_axes, y_count, rows_ref, src_ref, src_mass_ref, tgt_ref, own_ref, col_out, pot_out, own_src, kept
+    near, share_count, rows_ref, src_ref, src_mass_ref, tgt_ref, own_ref, col_out, pot_out, own_src, kept
 ):
-    merged, line = column_line(rows_ref, src_ref, src_mass_ref, tgt_ref, own_src, 256)
+    merged, line = column_line(rows_ref, src_ref, src_mass_ref, tgt_ref, own_src, 512)
     kept[...] = merged
-    mine = kept[pl.ds(lax.axis_index(x_axes), 1), :]
+    mine = kept[pl.ds(lax.axis_index(near), 1), :]
     coords = own_ref[...]
     norm = jnp.sum(coords * coords, axis=0, keepdims=True)
     pot_out[...] = 0.5 * norm - (2.0 * LN2) * mine
     pieces = as_rows(line)
-    share = len(pieces) // y_count
+    share = len(pieces) // share_count
     for to in range(col_out.shape[0]):
         for at in range(share):
-            col_out[to, at : at + 1, :] = pieces[(to % y_count) * share + at]
+            col_out[to, at : at + 1, :] = pieces[(to % share_count) * share + at]
 
 
 def final_kernel(cols_ref, tgt_ref, pot_out):
@@ -176,12 +186,13 @@
         pot_out[at : at + 1, :] = 0.5 * piece - (2.0 * LN2) * merged[at : at + 1, :]
 
 
-def call(kernel, outs, scratch=()):
+def call(kernel, outs, scratch=(), mib=24, **more):
     return pl.pallas_call(
         kernel,
         out_shape=outs,
+        **more,
         scratch_shapes=list(scratch),
-        compiler_params=pltpu.CompilerParams(vmem_limit_bytes=24 * 1024 * 1024),
+        compiler_params=pltpu.CompilerParams(vmem_limit_bytes=mib * 1024 * 1024),
     )
 
 
@@ -190,28 +201,33 @@
 
 
 def on_device(sources, log_source_mass, targets, log_target_mass, start_potential):
-    near, far = ("x", "c"), ("z", "y")
+    near, far = ("y", "x"), ("z", "c")
     dims, own_rows = sources.shape
     own_cols = targets.shape[1]
-    near_count, y_count = lax.axis_size(near), lax.axis_size("y")
+    near_count, share_count = lax.axis_size(near), lax.axis_size("c")
     far_count = lax.axis_size(far)
-    rows, cols = near_count * own_rows, y_count * own_cols
+    rows, cols = near_count * own_rows, share_count * own_cols
     row_tiles, col_tiles = rows // LANES, cols // LANES
     depth = len(LEFT) * ROWS
 
     def swap(value, axes):
         return lax.all_to_all(value, axes, 0, 0, tiled=True)
 
-    src_send, tgt_own = call(pack_kernel, (shape(near_count, ROWS, LANES), shape(ROWS, own_cols)))(
-        sources, log_source_mass[None], targets, log_target_mass[None], start_potential[None]
-    )
+    given = (sources, log_source_mass[None], targets, log_target_mass[None], start_potential[None])
+    src_send, tgt_own = call(
+        pack_kernel,
+        (shape(near_count, ROWS, LANES), shape(ROWS, own_cols)),
+        [pltpu.VMEM(array.shape, F32) for array in given] + [pltpu.SemaphoreType.DMA((len(given),))],
+        mib=60,
+        in_specs=[pl.BlockSpec(memory_space=pl.ANY)] * len(given),
+    )(*given)
     tgts = [tgt_own] + [
-        lax.ppermute(tgt_own, "y", [(k, (k + shift) % y_count) for k in range(y_count)])
-        for shift in range(1, y_count)
+        lax.ppermute(tgt_own, "c", [(k, (k + shift) % share_count) for k in range(share_count)])
+        for shift in range(1, share_count)
     ]
     src_all = swap(src_send, near)
     row_send, src, tgt, src_mass, tgt_mass = call(
-        functools.partial(first_kernel, dims, y_count),
+        functools.partial(first_kernel, dims, share_count),
         (
             shape(near_count, row_tiles, LANES),
             shape(depth, rows, dtype=BF16),
@@ -219,7 +235,7 @@
             shape(row_tiles, LANES),
             shape(col_tiles, LANES),
         ),
-        [pltpu.VMEM((y_count, ROWS, own_cols), F32)],
+        [pltpu.VMEM((share_count, ROWS, own_cols), F32)],
     )(src_all, *tgts)
     row_all = swap(row_send, near)
     col_send = call(
@@ -231,7 +247,7 @@
     )(col_all, src, tgt, tgt_mass)
     row_all = swap(row_send, near)
     col_send, row_potential = call(
-        functools.partial(last_column_kernel, near, y_count),
+        functools.partial(last_column_kernel, near, share_count),
         (shape(far_count, own_cols // LANES, LANES), shape(1, own_rows)),
         [pltpu.VMEM((depth, rows), BF16), pltpu.VMEM((row_tiles, LANES), F32)],
     )(row_all, src, src_mass, tgt, sources)

time: 81.5 us -> 78.5 us (0.963)
  the two profiles are of different devices: /device:TPU:2 before, /device:TPU:1 now
where the time goes in v2:
time: 78.5 us; the launch traced here: 78 us
  blocking collectives  50.2 us (64%)
  Pallas kernels  11.9 us (15%)
  starting transfers between devices  8.76 us (11%)
  waiting for transfers between devices  6.49 us (8%)
    all_to_all x4, blocking collectives, swap(): return lax.all_to_all(value, axes, 0, 0, tiled=True)  50.2 us
    all_to_all x1, starting transfers between devices, swap(): return lax.all_to_all(value, axes, 0, 0, tiled=True)  7.72 us
    all_to_all x1, waiting for transfers between devices, swap(): return lax.all_to_all(value, axes, 0, 0, tiled=True)  5.59 us
    pallas_call x1, Pallas kernels, on_device(): call(functools.partial(last_column_kernel, near, share_count), (shape(far...  2.85 us
    pallas_call x1, Pallas kernels, on_device(): call(column_kernel, shape(far_count, col_tiles, LANES), [pltpu.VMEM((dept...  2.42 us
    pallas_call x1, Pallas kernels, on_device(): call(functools.partial(first_kernel, dims, share_count), (shape(near_coun...  2.15 us
    pallas_call x1, Pallas kernels, on_device(): call(row_kernel, shape(near_count, row_tiles, LANES), [pltpu.VMEM((depth,...  2.13 us
    pallas_call x1, Pallas kernels, on_device(): call(pack_kernel, (shape(near_count, ROWS, LANES), shape(ROWS, own_cols))...  1.68 us
  transfers between devices with their start and end apart: 2, of which 2 were waited for; matrix products, arithmetic and copies ran while one was open for 0% of the time, Pallas kernels for 0%

profile of v2, /device:TPU:1, one launch (start us, length us, event | category | flops | bytes accessed | tf_op | source)
XLA Modules:
  0.0 78.0 jit_solution(13947139750223433514)
XLA Ops:
  0.6 1.7 %shard_map.68 = (f32[16,32,128]{2,1,0:T(8,128)}, f32[32,512]{1,0:T(8,128)}) custom-call(f32[30,128]{1,0:T(8,128)} %own_ref.1, f32[1,128]{1,0:T(1,128)} %bitcast.8, f32[30,512]{1,0:T(8,128)} %tgt_ref.1, f32[1,512]{1,0:T(1,128)} %bitcast.5, f32[1,512]{1,0:T(1,128)} %bitcast.6), custom_call_target="tpu_custom_call" | custom-call | tf_op jit(solution)/shard_map/pallas_call | solution.py:217
  2.3 0.0 copy-start.1
  2.3 7.7 %all-to-all-start = ((f32[16,32,128]{2,1,0:T(8,128)}), f32[16,32,128]{2,1,0:T(8,128)S(1)}, u32[]{:S(2)}, u32[]{:S(2)}) async-start(f32[16,32,128]{2,1,0:T(8,128)} %get-tuple-element.11), calls=%async_computation | async-start | bytes 524288 | tf_op jit(solution)/shard_map/all_to_all | solution.py:214
  10.0 0.0 copy-done.1
  10.1 1.0 %collective-permute-start = (f32[32,512]{1,0:T(8,128)S(1)}, f32[32,512]{1,0:T(8,128)S(1)}, u32[]{:S(2)}, u32[]{:S(2)}) collective-permute-start(f32[32,512]{1,0:T(8,128)S(1)} %copy-done.1), channel_id=1, source_target_pairs={{0,1},{1,0},{2,3},{3,2},{4,5},{5,4},{6,7},{7,6},{8,9},{9,8},{10,11... | collective-permute-start | bytes 196616 | tf_op jit(solution)/shard_map/ppermute | solution.py:225
  11.1 0.9 %collective-permute-done.refs_1_ = f32[32,512]{1,0:T(8,128)S(1)} collective-permute-done((f32[32,512]{1,0:T(8,128)S(1)}, f32[32,512]{1,0:T(8,128)S(1)}, u32[]{:S(2)}, u32[]{:S(2)}) %collective-permute-start) | collective-permute-done | bytes 65568 | tf_op jit(solution)/shard_map/ppermute | solution.py:225
  12.0 5.6 %all-to-all-done.src_ref = f32[16,32,128]{2,1,0:T(8,128)S(1)} async-done(((f32[16,32,128]{2,1,0:T(8,128)}), f32[16,32,128]{2,1,0:T(8,128)S(1)}, u32[]{:S(2)}, u32[]{:S(2)}) %all-to-all-start) | async-done | bytes 262176 | tf_op jit(solution)/shard_map/all_to_all | solution.py:214
  17.6 2.1 %shard_map.69 = (f32[16,16,128]{2,1,0:T(8,128)S(1)}, bf16[192,2048]{1,0:T(8,128)(2,1)S(1)}, bf16[192,1024]{1,0:T(8,128)(2,1)S(1)}, f32[16,128]{1,0:T(8,128)S(1)}, f32[8,128]{1,0:T(8,128)S(1)}) custom-call(f32[16,32,128]{2,1,0:T(8,128)S(1)} %all-to-all-done.src_ref, f32[32,512]{1,0:T(8,128)S(1)} %copy-done.1, f32[32,512]{1,0:T(8,128)S(1)} %collective-permute-done.refs_1_), custom_call_target="tpu_custom_call" | custom-call | tf_op jit(solution)/shard_map/pallas_call | solution.py:229
  19.7 9.7 %all_to_all.25.rows_ref = f32[16,16,128]{2,1,0:T(8,128)S(1)} all-to-all(f32[16,16,128]{2,1,0:T(8,128)S(1)} %get-tuple-element.13), channel_id=1, replica_groups=mesh['z'=8,'y'=4,'x'=4,'c'=2] {'y','x'}, dimensions={0} | all-to-all | bytes 262144 | tf_op jit(solution)/shard_map/all_to_all | solution.py:214
  29.5 2.4 %shard_map.70 = f32[16,8,128]{2,1,0:T(8,128)S(1)} custom-call(f32[16,16,128]{2,1,0:T(8,128)S(1)} %all_to_all.25.rows_ref, bf16[192,2048]{1,0:T(8,128)(2,1)S(1)} %get-tuple-element.14.src_ref, f32[16,128]{1,0:T(8,128)S(1)} %get-tuple-element.15.src_mass_ref, bf16[192,1024]{1,0:T(8,128)(2,1)S(1)} %get-tuple-element.16.tgt_ref), custom_call_target="tpu_custom_call" | custom-call | tf_op jit(solution)/shard_map/pallas_call | solution.py:241
  31.9 19.3 %all_to_all.26.cols_ref = f32[16,8,128]{2,1,0:T(8,128)S(1)} all-to-all(f32[16,8,128]{2,1,0:T(8,128)S(1)} %shard_map.70), channel_id=1, replica_groups=mesh['z'=8,'y'=4,'x'=4,'c'=2] {'z','c'}, dimensions={0} | all-to-all | bytes 131072 | tf_op jit(solution)/shard_map/all_to_all | solution.py:214
  51.2 2.1 %shard_map.71 = f32[16,16,128]{2,1,0:T(8,128)S(1)} custom-call(f32[16,8,128]{2,1,0:T(8,128)S(1)} %all_to_all.26.cols_ref, bf16[192,2048]{1,0:T(8,128)(2,1)S(1)} %get-tuple-element.14.src_ref, bf16[192,1024]{1,0:T(8,128)(2,1)S(1)} %get-tuple-element.16.tgt_ref, f32[8,128]{1,0:T(8,128)S(1)} %get-tuple-element.17.tgt_mass_ref), custom_call_target="tpu_custom_call" | custom-call | tf_op jit(solution)/shard_map/pallas_call | solution.py:245
  53.3 0.0 copy-start.2
  53.3 9.7 %all_to_all.27.rows_ref = f32[16,16,128]{2,1,0:T(8,128)S(1)} all-to-all(f32[16,16,128]{2,1,0:T(8,128)S(1)} %shard_map.71), channel_id=1, replica_groups=mesh['z'=8,'y'=4,'x'=4,'c'=2] {'y','x'}, dimensions={0} | all-to-all | bytes 262144 | tf_op jit(solution)/shard_map/all_to_all | solution.py:214
  63.0 0.0 copy-done.2
  63.0 2.9 %shard_map.72 = (f32[16,4,128]{2,1,0:T(4,128)S(1)}, f32[1,128]{1,0:T(1,128)}) custom-call(f32[16,16,128]{2,1,0:T(8,128)S(1)} %all_to_all.27.rows_ref, bf16[192,2048]{1,0:T(8,128)(2,1)S(1)} %get-tuple-element.14.src_ref, f32[16,128]{1,0:T(8,128)S(1)} %get-tuple-element.15.src_mass_ref, bf16[192,1024]{1,0:T(8,128)(2,1)S(1)} %get-tuple-element.16.tgt_ref, ...), custom_call_target="tpu_custom_call" | custom-call | tf_op jit(solution)/shard_map/pallas_call | solution.py:249
  65.8 0.0 copy-start
  65.8 11.5 %all_to_all.28.cols_ref = f32[16,4,128]{2,1,0:T(4,128)S(1)} all-to-all(f32[16,4,128]{2,1,0:T(4,128)S(1)} %get-tuple-element.19), channel_id=1, replica_groups=mesh['z'=8,'y'=4,'x'=4,'c'=2] {'z','c'}, dimensions={0} | all-to-all | bytes 65536 | tf_op jit(solution)/shard_map/all_to_all | solution.py:214
  77.4 0.0 copy-done
  77.4 0.6 shard_map.73
Async XLA Ops:
  2.3 7.7 %copy-start.1 = (f32[32,512]{1,0:T(8,128)S(1)}, f32[32,512]{1,0:T(8,128)}, u32[]{:S(2)}) copy-start(f32[32,512]{1,0:T(8,128)} %get-tuple-element.12.refs_0_) | copy-start | bytes 196612
  2.3 15.3 %all-to-all-start = ((f32[16,32,128]{2,1,0:T(8,128)}), f32[16,32,128]{2,1,0:T(8,128)S(1)}, u32[]{:S(2)}, u32[]{:S(2)}) async-start(f32[16,32,128]{2,1,0:T(8,128)} %get-tuple-element.11), calls=%async_computation | async-start | bytes 524288 | tf_op jit(solution)/shard_map/all_to_all | solution.py:214
  10.1 1.9 %collective-permute-start = (f32[32,512]{1,0:T(8,128)S(1)}, f32[32,512]{1,0:T(8,128)S(1)}, u32[]{:S(2)}, u32[]{:S(2)}) collective-permute-start(f32[32,512]{1,0:T(8,128)S(1)} %copy-done.1), channel_id=1, source_target_pairs={{0,1},{1,0},{2,3},{3,2},{4,5},{5,4},{6,7},{7,6},{8,9},{9,8},{10,11... | collective-permute-start | bytes 196616 | tf_op jit(solution)/shard_map/ppermute | solution.py:225
  53.3 9.7 %copy-start.2 = (f32[30,128]{1,0:T(8,128)S(1)}, f32[30,128]{1,0:T(8,128)}, u32[]{:S(2)}) copy-start(f32[30,128]{1,0:T(8,128)} %own_ref.1) | copy-start | bytes 46084
  65.8 11.5 %copy-start = (f32[30,512]{1,0:T(8,128)S(1)}, f32[30,512]{1,0:T(8,128)}, u32[]{:S(2)}) copy-start(f32[30,512]{1,0:T(8,128)} %tgt_ref.1) | copy-start | bytes 184324

commit v3 on v2

--- a/solution.py
+++ b/solution.py
@@ -12,10 +12,11 @@
 LOG2E = math.log2(math.e)
 LN2 = math.log(2.0)
 LANES = 128
+TILE = 256
+STEP = 128
 ROWS = 32
 LEFT = (0, 0, 1, 1, 0, 2)
 RIGHT = (0, 1, 0, 1, 2, 0)
-LOWEST = -1e30
 F32, BF16 = jnp.float32, jnp.bfloat16
 
 
@@ -40,23 +41,39 @@
     return jnp.where(row_of(block.shape, row), value, block)
 
 
-def fold(left_ref, right_ref, step):
-    count, width = left_ref.shape[1], right_ref.shape[1]
-    peak = jnp.full((8, width), LOWEST, F32)
-    total = jnp.zeros((8, width), F32)
-    for at in range(0, count, step):
-        scores = lax.dot_general(
-            left_ref[:, at : at + step],
-            right_ref[...],
+def fold(left, count, right_ref, step=STEP, tile=TILE):
+    items = [(lane, at) for lane in range(0, right_ref.shape[1], tile) for at in range(0, count, step)]
+
+    def scores_of(lane, at):
+        return lax.dot_general(
+            left(slice(at, at + step)),
+            right_ref[:, lane : lane + tile],
             (((0,), (0,)), ((), ())),
             preferred_element_type=F32,
-        ).reshape(step // 8, 8, width)
-        new_peak = jnp.maximum(peak, jnp.max(scores, axis=0))
-        total = total * jnp.exp2(peak - new_peak) + jnp.sum(jnp.exp2(scores - new_peak[None]), axis=0)
-        peak = new_peak
-    top = jnp.max(peak, axis=0, keepdims=True)
-    whole = jnp.sum(total * jnp.exp2(peak - top), axis=0, keepdims=True)
-    return top + LOG2E * jnp.log(whole)
+        ).reshape(step // 8, 8, tile)
+
+    lines = []
+    coming = scores_of(*items[0])
+    for number, (lane, at) in enumerate(items):
+        scores = coming
+        if number + 1 < len(items):
+            coming = scores_of(*items[number + 1])
+        if at == 0:
+            peak = jnp.max(scores, axis=0)
+            total = jnp.sum(jnp.exp2(scores - peak[None]), axis=0)
+        else:
+            new_peak = jnp.maximum(peak, jnp.max(scores, axis=0))
+            total = total * jnp.exp2(peak - new_peak) + jnp.sum(jnp.exp2(scores - new_peak[None]), axis=0)
+            peak = new_peak
+        if at + step == count:
+            top = jnp.max(peak, axis=0, keepdims=True)
+            whole = jnp.sum(total * jnp.exp2(peak - top), axis=0, keepdims=True)
+            lines.append(top + LOG2E * jnp.log(whole))
+    return jnp.concatenate(lines, axis=1)
+
+
+def patched(own_ref, ref):
+    return lambda lanes: jnp.concatenate([own_ref[:, lanes], ref[own_ref.shape[0] :, lanes]], axis=0)
 
 
 def as_rows(line):
@@ -82,14 +99,6 @@
     tgt_out[...] = jnp.concatenate([tgt, tgt_mass, start], axis=0)
     block = jnp.concatenate([src, src_mass, jnp.zeros((1, LANES), F32)], axis=0)
     src_out[...] = jnp.broadcast_to(block[None], src_out.shape)
-
-
-def set_beta(tgt_ref, at, beta):
-    lanes = slice(at, at + beta.shape[1])
-    for slot, part in enumerate(parts_of(beta)):
-        rows = slice(slot * ROWS, slot * ROWS + ROWS)
-        block = tgt_ref[rows, lanes].astype(F32)
-        tgt_ref[rows, lanes] = with_row(block, ROWS - 2, part.astype(F32)).astype(BF16)
 
 
 def first_kernel(dims, share_count, src_ref, *refs):
@@ -131,54 +140,51 @@
                 piece = with_row(piece, ROWS - 2, beta_parts[slot].astype(F32))
                 piece = with_row(piece, ROWS - 1, 1.0)
             tgt_out[slot * ROWS : slot * ROWS + ROWS, lanes] = piece.astype(BF16)
-    send_to_all(fold(tgt_out, src_out, 256), row_out)
-
-
-def column_line(rows_ref, src_ref, src_mass_ref, tgt_ref, own_src, step):
-    merged = merge(rows_ref[...])
-    alpha = src_mass_ref[...] - merged
-    split = parts_of(alpha)
-    own_src[...] = src_ref[...]
-    for group in range(alpha.shape[0]):
+    send_to_all(fold(lambda lanes: tgt_out[:, lanes], tgt_out.shape[1], src_out), row_out)
+
+
+def set_terms(own_ref, ref, values, cleared, row):
+    split = parts_of(values)
+    for group in range(values.shape[0]):
         lanes = slice(group * LANES, group * LANES + LANES)
         for slot in range(3):
             rows = slice(slot * ROWS, slot * ROWS + ROWS)
-            block = with_row(src_ref[rows, lanes].astype(F32), ROWS - 2, 0.0)
-            value = split[slot][group : group + 1, :].astype(F32)
-            own_src[rows, lanes] = with_row(block, ROWS - 1, value).astype(BF16)
-    return merged, fold(own_src, tgt_ref, step)
+            block = ref[rows, lanes].astype(F32)
+            if cleared is not None:
+                block = with_row(block, cleared, 0.0)
+            own_ref[rows, lanes] = with_row(block, row, split[slot][group : group + 1, :].astype(F32)).astype(BF16)
+
+
+def column_line(merged, src_ref, src_mass_ref, tgt_ref, own_src):
+    set_terms(own_src, src_ref, src_mass_ref[...] - merged, ROWS - 2, ROWS - 1)
+    return fold(patched(own_src, src_ref), src_ref.shape[1], tgt_ref)
 
 
 def column_kernel(rows_ref, src_ref, src_mass_ref, tgt_ref, col_out, own_src):
-    _, line = column_line(rows_ref, src_ref, src_mass_ref, tgt_ref, own_src, 512)
-    send_to_all(line, col_out)
+    send_to_all(column_line(merge(rows_ref[...]), src_ref, src_mass_ref, tgt_ref, own_src), col_out)
 
 
 def row_kernel(cols_ref, src_ref, tgt_ref, tgt_mass_ref, row_out, own_tgt):
-    beta = tgt_mass_ref[...] - merge(cols_ref[...])
-    own_tgt[...] = tgt_ref[...]
-    for group in range(beta.shape[0]):
-        set_beta(own_tgt, group * LANES, beta[group : group + 1, :])
-    send_to_all(fold(own_tgt, src_ref, 256), row_out)
-
-
-def last_column_kernel(
-    near, share_count, rows_ref, src_ref, src_mass_ref, tgt_ref, own_ref, col_out, pot_out, own_src, kept
-):
-    merged, line = column_line(rows_ref, src_ref, src_mass_ref, tgt_ref, own_src, 512)
-    kept[...] = merged
-    mine = kept[pl.ds(lax.axis_index(near), 1), :]
-    coords = own_ref[...]
+    set_terms(own_tgt, tgt_ref, tgt_mass_ref[...] - merge(cols_ref[...]), None, ROWS - 2)
+    send_to_all(fold(patched(own_tgt, tgt_ref), tgt_ref.shape[1], src_ref), row_out)
+
+
+def last_column_kernel(share_count, rows_ref, src_ref, src_mass_ref, tgt_ref, col_out, merged_out, own_src):
+    merged = merge(rows_ref[...])
+    merged_out[...] = merged
+    pieces = as_rows(column_line(merged, src_ref, src_mass_ref, tgt_ref, own_src))
+    share = len(pieces) // share_count
+    for part in range(share_count):
+        block = jnp.concatenate(pieces[part * share : part * share + share], axis=0)
+        for to in range(part, col_out.shape[0], share_count):
+            col_out[to] = block
+
+
+def final_kernel(near, cols_ref, rows_ref, src_ref, tgt_ref, row_out, pot_out):
+    mine = rows_ref[pl.ds(lax.axis_index(near), 1), :]
+    coords = src_ref[...]
     norm = jnp.sum(coords * coords, axis=0, keepdims=True)
-    pot_out[...] = 0.5 * norm - (2.0 * LN2) * mine
-    pieces = as_rows(line)
-    share = len(pieces) // share_count
-    for to in range(col_out.shape[0]):
-        for at in range(share):
-            col_out[to, at : at + 1, :] = pieces[(to % share_count) * share + at]
-
-
-def final_kernel(cols_ref, tgt_ref, pot_out):
+    row_out[...] = 0.5 * norm - (2.0 * LN2) * mine
     merged = merge(cols_ref[...])
     coords = tgt_ref[...]
     norm = jnp.sum(coords * coords, axis=0, keepdims=True)
@@ -218,9 +224,8 @@
         pack_kernel,
         (shape(near_count, ROWS, LANES), shape(ROWS, own_cols)),
         [pltpu.VMEM(array.shape, F32) for array in given] + [pltpu.SemaphoreType.DMA((len(given),))],
-        mib=60,
         in_specs=[pl.BlockSpec(memory_space=pl.ANY)] * len(given),
-    )(*given)
+    )(*[pltpu.with_memory_space_constraint(array, pltpu.HBM) for array in given])
     tgts = [tgt_own] + [
         lax.ppermute(tgt_own, "c", [(k, (k + shift) % share_count) for k in range(share_count)])
         for shift in range(1, share_count)
@@ -237,22 +242,25 @@
         ),
         [pltpu.VMEM((share_count, ROWS, own_cols), F32)],
     )(src_all, *tgts)
+    changed = 3 * ROWS
     row_all = swap(row_send, near)
     col_send = call(
-        column_kernel, shape(far_count, col_tiles, LANES), [pltpu.VMEM((depth, rows), BF16)]
+        column_kernel, shape(far_count, col_tiles, LANES), [pltpu.VMEM((changed, rows), BF16)]
     )(row_all, src, src_mass, tgt)
     col_all = swap(col_send, far)
     row_send = call(
-        row_kernel, shape(near_count, row_tiles, LANES), [pltpu.VMEM((depth, cols), BF16)]
+        row_kernel, shape(near_count, row_tiles, LANES), [pltpu.VMEM((changed, cols), BF16)]
     )(col_all, src, tgt, tgt_mass)
     row_all = swap(row_send, near)
-    col_send, row_potential = call(
-        functools.partial(last_column_kernel, near, share_count),
-        (shape(far_count, own_cols // LANES, LANES), shape(1, own_rows)),
-        [pltpu.VMEM((depth, rows), BF16), pltpu.VMEM((row_tiles, LANES), F32)],
-    )(row_all, src, src_mass, tgt, sources)
+    col_send, merged = call(
+        functools.partial(last_column_kernel, share_count),
+        (shape(far_count, own_cols // LANES, LANES), shape(row_tiles, LANES)),
+        [pltpu.VMEM((changed, rows), BF16)],
+    )(row_all, src, src_mass, tgt)
     col_all = swap(col_send, far)
-    column_potential = call(final_kernel, shape(own_cols // LANES, LANES))(col_all, targets)
+    row_potential, column_potential = call(
+        functools.partial(final_kernel, near), (shape(1, own_rows), shape(own_cols // LANES, LANES))
+    )(col_all, merged, sources, targets)
     return row_potential.reshape(own_rows), column_potential.reshape(own_cols)
 
 

time: 78.5 us -> 76.3 us (0.972)
  Pallas kernels: 11.9 us -> 9.84 us
    pallas_call x4, Pallas kernels: 8.03 us -> 6.14 us  [the longest x1 1.88 us: on_device(): call(row_kernel, shape(near_count, row_tiles, LANES), [pltpu.VMEM((change...]
where the time goes in v3:
time: 76.3 us; the launch traced here: 75.9 us
  blocking collectives  50.2 us (66%)
  Pallas kernels  9.84 us (13%)
  starting transfers between devices  8.63 us (11%)
  waiting for transfers between devices  6.5 us (9%)
    all_to_all x4, blocking collectives, swap(): return lax.all_to_all(value, axes, 0, 0, tiled=True)  50.2 us
    all_to_all x1, starting transfers between devices, swap(): return lax.all_to_all(value, axes, 0, 0, tiled=True)  7.58 us
    all_to_all x1, waiting for transfers between devices, swap(): return lax.all_to_all(value, axes, 0, 0, tiled=True)  5.6 us
    pallas_call x1, Pallas kernels, on_device(): call(functools.partial(first_kernel, dims, share_count), (shape(near_coun...  2.05 us
    pallas_call x1, Pallas kernels, on_device(): call(row_kernel, shape(near_count, row_tiles, LANES), [pltpu.VMEM((change...  1.88 us
    pallas_call x1, Pallas kernels, on_device(): call(column_kernel, shape(far_count, col_tiles, LANES), [pltpu.VMEM((chan...  1.84 us
    pallas_call x1, Pallas kernels, on_device(): call(functools.partial(last_column_kernel, share_count), (shape(far_count...  1.79 us
    pallas_call x1, Pallas kernels, on_device(): call(pack_kernel, (shape(near_count, ROWS, LANES), shape(ROWS, own_cols))...  1.64 us
  transfers between devices with their start and end apart: 2, of which 2 were waited for; matrix products, arithmetic and copies ran while one was open for 0% of the time, Pallas kernels for 0%

profile of v3, /device:TPU:1, one launch (start us, length us, event | category | flops | bytes accessed | tf_op | source)
XLA Modules:
  0.0 75.9 jit_solution(15222260227258026892)
XLA Ops:
  0.6 1.6 %shard_map.68 = (f32[16,32,128]{2,1,0:T(8,128)}, f32[32,512]{1,0:T(8,128)S(1)}) custom-call(f32[30,128]{1,0:T(8,128)} %src_ref.1, f32[1,128]{1,0:T(1,128)} %bitcast.7, f32[30,512]{1,0:T(8,128)} %tgt_ref.1, f32[1,512]{1,0:T(1,128)} %bitcast.5, f32[1,512]{1,0:T(1,128)} %bitcast.6), custom_call_target="tpu_custom_call" | custom-call | tf_op jit(solution)/shard_map/pallas_call | solution.py:223
  2.3 7.6 %all-to-all-start = ((f32[16,32,128]{2,1,0:T(8,128)}), f32[16,32,128]{2,1,0:T(8,128)S(1)}, u32[]{:S(2)}, u32[]{:S(2)}) async-start(f32[16,32,128]{2,1,0:T(8,128)} %get-tuple-element.13), calls=%async_computation | async-start | bytes 524288 | tf_op jit(solution)/shard_map/all_to_all | solution.py:220
  9.9 1.0 %collective-permute-start = (f32[32,512]{1,0:T(8,128)S(1)}, f32[32,512]{1,0:T(8,128)S(1)}, u32[]{:S(2)}, u32[]{:S(2)}) collective-permute-start(f32[32,512]{1,0:T(8,128)S(1)} %get-tuple-element.14.refs_0_), channel_id=1, source_target_pairs={{0,1},{1,0},{2,3},{3,2},{4,5},{5,4},{6,7},{7,6},{8,9},{9,8},{10,11... | collective-permute-start | bytes 196616 | tf_op jit(solution)/shard_map/ppermute | solution.py:230
  10.9 0.9 %collective-permute-done.refs_1_ = f32[32,512]{1,0:T(8,128)S(1)} collective-permute-done((f32[32,512]{1,0:T(8,128)S(1)}, f32[32,512]{1,0:T(8,128)S(1)}, u32[]{:S(2)}, u32[]{:S(2)}) %collective-permute-start) | collective-permute-done | bytes 65568 | tf_op jit(solution)/shard_map/ppermute | solution.py:230
  11.8 5.6 %all-to-all-done.src_ref = f32[16,32,128]{2,1,0:T(8,128)S(1)} async-done(((f32[16,32,128]{2,1,0:T(8,128)}), f32[16,32,128]{2,1,0:T(8,128)S(1)}, u32[]{:S(2)}, u32[]{:S(2)}) %all-to-all-start) | async-done | bytes 262176 | tf_op jit(solution)/shard_map/all_to_all | solution.py:220
  17.4 2.1 %shard_map.69 = (f32[16,16,128]{2,1,0:T(8,128)S(1)}, bf16[192,2048]{1,0:T(8,128)(2,1)S(1)}, bf16[192,1024]{1,0:T(8,128)(2,1)S(1)}, f32[16,128]{1,0:T(8,128)S(1)}, f32[8,128]{1,0:T(8,128)S(1)}) custom-call(f32[16,32,128]{2,1,0:T(8,128)S(1)} %all-to-all-done.src_ref, f32[32,512]{1,0:T(8,128)S(1)} %get-tuple-element.14.refs_0_, ...), custom_call_target="tpu_custom_call" | custom-call | tf_op jit(solution)/shard_map/pallas_call | solution.py:234
  19.5 9.8 %all_to_all.25.rows_ref = f32[16,16,128]{2,1,0:T(8,128)S(1)} all-to-all(f32[16,16,128]{2,1,0:T(8,128)S(1)} %get-tuple-element.15), channel_id=1, replica_groups=mesh['z'=8,'y'=4,'x'=4,'c'=2] {'y','x'}, dimensions={0} | all-to-all | bytes 262144 | tf_op jit(solution)/shard_map/all_to_all | solution.py:220
  29.2 1.8 %shard_map.70 = f32[16,8,128]{2,1,0:T(8,128)S(1)} custom-call(f32[16,16,128]{2,1,0:T(8,128)S(1)} %all_to_all.25.rows_ref, bf16[192,2048]{1,0:T(8,128)(2,1)S(1)} %get-tuple-element.16.src_ref, f32[16,128]{1,0:T(8,128)S(1)} %get-tuple-element.17.src_mass_ref, bf16[192,1024]{1,0:T(8,128)(2,1)S(1)} %get-tuple-element.18.tgt_ref), custom_call_target="tpu_custom_call" | custom-call | tf_op jit(solution)/shard_map/pallas_call | solution.py:247
  31.1 19.3 %all_to_all.26.cols_ref = f32[16,8,128]{2,1,0:T(8,128)S(1)} all-to-all(f32[16,8,128]{2,1,0:T(8,128)S(1)} %shard_map.70), channel_id=1, replica_groups=mesh['z'=8,'y'=4,'x'=4,'c'=2] {'z','c'}, dimensions={0} | all-to-all | bytes 131072 | tf_op jit(solution)/shard_map/all_to_all | solution.py:220
  50.4 1.9 %shard_map.71 = f32[16,16,128]{2,1,0:T(8,128)S(1)} custom-call(f32[16,8,128]{2,1,0:T(8,128)S(1)} %all_to_all.26.cols_ref, bf16[192,2048]{1,0:T(8,128)(2,1)S(1)} %get-tuple-element.16.src_ref, bf16[192,1024]{1,0:T(8,128)(2,1)S(1)} %get-tuple-element.18.tgt_ref, f32[8,128]{1,0:T(8,128)S(1)} %get-tuple-element.19.tgt_mass_ref), custom_call_target="tpu_custom_call" | custom-call | tf_op jit(solution)/shard_map/pallas_call | solution.py:251
  52.2 9.6 %all_to_all.27.rows_ref = f32[16,16,128]{2,1,0:T(8,128)S(1)} all-to-all(f32[16,16,128]{2,1,0:T(8,128)S(1)} %shard_map.71), channel_id=1, replica_groups=mesh['z'=8,'y'=4,'x'=4,'c'=2] {'y','x'}, dimensions={0} | all-to-all | bytes 262144 | tf_op jit(solution)/shard_map/all_to_all | solution.py:220
  61.9 0.0 copy-start.1
  61.9 1.8 %shard_map.72 = (f32[16,4,128]{2,1,0:T(4,128)S(1)}, f32[16,128]{1,0:T(8,128)S(1)}) custom-call(f32[16,16,128]{2,1,0:T(8,128)S(1)} %all_to_all.27.rows_ref, bf16[192,2048]{1,0:T(8,128)(2,1)S(1)} %get-tuple-element.16.src_ref, f32[16,128]{1,0:T(8,128)S(1)} %get-tuple-element.17.src_mass_ref, bf16[192,1024]{1,0:T(8,128)(2,1)S(1)} %get-tuple-element.18.tgt_ref), custom_call_target="tpu_custom_call" | custom-call | tf_op jit(solution)/shard_map/pallas_call | solution.py:255
  63.7 0.0 copy-start
  63.7 11.6 %all_to_all.28.cols_ref = f32[16,4,128]{2,1,0:T(4,128)S(1)} all-to-all(f32[16,4,128]{2,1,0:T(4,128)S(1)} %get-tuple-element.20), channel_id=1, replica_groups=mesh['z'=8,'y'=4,'x'=4,'c'=2] {'z','c'}, dimensions={0} | all-to-all | bytes 65536 | tf_op jit(solution)/shard_map/all_to_all | solution.py:220
  75.2 0.0 copy-done.1
  75.2 0.0 copy-done
  75.3 0.6 shard_map.73
Async XLA Ops:
  2.3 15.1 %all-to-all-start = ((f32[16,32,128]{2,1,0:T(8,128)}), f32[16,32,128]{2,1,0:T(8,128)S(1)}, u32[]{:S(2)}, u32[]{:S(2)}) async-start(f32[16,32,128]{2,1,0:T(8,128)} %get-tuple-element.13), calls=%async_computation | async-start | bytes 524288 | tf_op jit(solution)/shard_map/all_to_all | solution.py:220
  9.9 1.9 %collective-permute-start = (f32[32,512]{1,0:T(8,128)S(1)}, f32[32,512]{1,0:T(8,128)S(1)}, u32[]{:S(2)}, u32[]{:S(2)}) collective-permute-start(f32[32,512]{1,0:T(8,128)S(1)} %get-tuple-element.14.refs_0_), channel_id=1, source_target_pairs={{0,1},{1,0},{2,3},{3,2},{4,5},{5,4},{6,7},{7,6},{8,9},{9,8},{10,11... | collective-permute-start | bytes 196616 | tf_op jit(solution)/shard_map/ppermute | solution.py:230
  61.9 13.4 %copy-start.1 = (f32[30,128]{1,0:T(8,128)S(1)}, f32[30,128]{1,0:T(8,128)}, u32[]{:S(2)}) copy-start(f32[30,128]{1,0:T(8,128)} %src_ref.1) | copy-start | bytes 46084
  63.7 11.6 %copy-start = (f32[30,512]{1,0:T(8,128)S(1)}, f32[30,512]{1,0:T(8,128)}, u32[]{:S(2)}) copy-start(f32[30,512]{1,0:T(8,128)} %tgt_ref.1) | copy-start | bytes 184324

commit v4 on v3

--- a/solution.py
+++ b/solution.py
@@ -14,6 +14,8 @@
 LANES = 128
 TILE = 256
 STEP = 128
+PLAN_STEP = 512
+SMALLEST = 2.0**-90
 ROWS = 32
 LEFT = (0, 0, 1, 1, 0, 2)
 RIGHT = (0, 1, 0, 1, 2, 0)
@@ -41,13 +43,13 @@
     return jnp.where(row_of(block.shape, row), value, block)
 
 
-def fold(left, count, right_ref, step=STEP, tile=TILE):
-    items = [(lane, at) for lane in range(0, right_ref.shape[1], tile) for at in range(0, count, step)]
+def fold(left, count, right, width, step=STEP, tile=TILE):
+    items = [(lane, at) for lane in range(0, width, tile) for at in range(0, count, step)]
 
     def scores_of(lane, at):
         return lax.dot_general(
             left(slice(at, at + step)),
-            right_ref[:, lane : lane + tile],
+            right(slice(lane, lane + tile)),
             (((0,), (0,)), ((), ())),
             preferred_element_type=F32,
         ).reshape(step // 8, 8, tile)
@@ -72,12 +74,43 @@
     return jnp.concatenate(lines, axis=1)
 
 
+def plan_line(left, count, right, width, line_ref):
+    lines = []
+    for lane in range(0, width, TILE):
+        total = jnp.zeros((8, TILE), F32)
+        for at in range(0, count, PLAN_STEP):
+            scores = lax.dot_general(
+                left(slice(at, at + PLAN_STEP)),
+                right(slice(lane, lane + TILE)),
+                (((0,), (0,)), ((), ())),
+                preferred_element_type=F32,
+            ).reshape(PLAN_STEP // 8, 8, TILE)
+            total = total + jnp.sum(jnp.exp2(scores), axis=0)
+        lines.append(jnp.sum(total, axis=0, keepdims=True))
+    set_rows(line_ref, jnp.concatenate(lines, axis=1), 0)
+    sums = line_ref[...]
+    line_ref[...] = LOG2E * jnp.log(sums)
+
+    @pl.when(jnp.min(sums) < SMALLEST)
+    def again():
+        set_rows(line_ref, fold(left, count, right, width), 0)
+
+
+def whole(ref):
+    return lambda lanes: ref[:, lanes]
+
+
 def patched(own_ref, ref):
     return lambda lanes: jnp.concatenate([own_ref[:, lanes], ref[own_ref.shape[0] :, lanes]], axis=0)
 
 
 def as_rows(line):
     return [line[:, at : at + LANES] for at in range(0, line.shape[1], LANES)]
+
+
+def set_rows(ref, line, row):
+    for at, piece in enumerate(as_rows(line)):
+        ref[row + at : row + at + 1, :] = piece
 
 
 def send_to_all(line, out_ref):
@@ -103,8 +136,8 @@
 
 def first_kernel(dims, share_count, src_ref, *refs):
     tgt_refs = refs[:share_count]
-    row_out, src_out, tgt_out, src_mass_out, tgt_mass_out = refs[share_count : share_count + 5]
-    held = refs[share_count + 5]
+    row_out, src_out, tgt_out, src_mass_out, tgt_mass_out, beta_out = refs[share_count : share_count + 6]
+    held = refs[share_count + 6]
     mine = lax.axis_index("c")
     for shift in range(share_count):
         held[lax.rem(mine + share_count - shift, share_count)] = tgt_refs[shift][...]
@@ -124,14 +157,13 @@
     for group in range(share_count):
         block = held[group]
         mass = LOG2E * block[dims : dims + 1, :]
-        for at, piece in enumerate(as_rows(mass)):
-            row = group * (width // LANES) + at
-            tgt_mass_out[row : row + 1, :] = piece
+        set_rows(tgt_mass_out, mass, group * (width // LANES))
         spare = lax.broadcasted_iota(jnp.int32, block.shape, 0) >= dims
         coords = jnp.where(spare, 0.0, block)
         split = parts_of(coords)
         norm = jnp.sum(coords * coords, axis=0, keepdims=True)
         beta = mass + LOG2E * (0.5 * block[dims + 1 : dims + 2, :] - 0.25 * norm)
+        set_rows(beta_out, beta, group * (width // LANES))
         beta_parts = parts_of(beta)
         lanes = slice(group * width, group * width + width)
         for slot, which in enumerate(RIGHT):
@@ -140,44 +172,53 @@
                 piece = with_row(piece, ROWS - 2, beta_parts[slot].astype(F32))
                 piece = with_row(piece, ROWS - 1, 1.0)
             tgt_out[slot * ROWS : slot * ROWS + ROWS, lanes] = piece.astype(BF16)
-    send_to_all(fold(lambda lanes: tgt_out[:, lanes], tgt_out.shape[1], src_out), row_out)
-
-
-def set_terms(own_ref, ref, values, cleared, row):
+    send_to_all(fold(whole(tgt_out), tgt_out.shape[1], whole(src_out), src_out.shape[1]), row_out)
+
+
+def set_terms(own_ref, ref, values, row):
     split = parts_of(values)
     for group in range(values.shape[0]):
         lanes = slice(group * LANES, group * LANES + LANES)
         for slot in range(3):
             rows = slice(slot * ROWS, slot * ROWS + ROWS)
             block = ref[rows, lanes].astype(F32)
-            if cleared is not None:
-                block = with_row(block, cleared, 0.0)
             own_ref[rows, lanes] = with_row(block, row, split[slot][group : group + 1, :].astype(F32)).astype(BF16)
 
 
-def column_line(merged, src_ref, src_mass_ref, tgt_ref, own_src):
-    set_terms(own_src, src_ref, src_mass_ref[...] - merged, ROWS - 2, ROWS - 1)
-    return fold(patched(own_src, src_ref), src_ref.shape[1], tgt_ref)
-
-
-def column_kernel(rows_ref, src_ref, src_mass_ref, tgt_ref, col_out, own_src):
-    send_to_all(column_line(merge(rows_ref[...]), src_ref, src_mass_ref, tgt_ref, own_src), col_out)
-
-
-def row_kernel(cols_ref, src_ref, tgt_ref, tgt_mass_ref, row_out, own_tgt):
-    set_terms(own_tgt, tgt_ref, tgt_mass_ref[...] - merge(cols_ref[...]), None, ROWS - 2)
-    send_to_all(fold(patched(own_tgt, tgt_ref), tgt_ref.shape[1], src_ref), row_out)
-
-
-def last_column_kernel(share_count, rows_ref, src_ref, src_mass_ref, tgt_ref, col_out, merged_out, own_src):
+def column_kernel(rows_ref, src_ref, src_mass_ref, tgt_ref, beta_ref, col_out, alpha_out, own_src, line_ref):
+    alpha = src_mass_ref[...] - merge(rows_ref[...])
+    alpha_out[...] = alpha
+    set_terms(own_src, src_ref, alpha, ROWS - 1)
+    plan_line(patched(own_src, src_ref), src_ref.shape[1], whole(tgt_ref), tgt_ref.shape[1], line_ref)
+    col_out[...] = jnp.broadcast_to((line_ref[...] - beta_ref[...])[None], col_out.shape)
+
+
+def row_kernel(
+    cols_ref, own_src, src_ref, tgt_ref, tgt_mass_ref, alpha_ref, row_out, own_tgt, beta_out, line_ref
+):
+    beta = tgt_mass_ref[...] - merge(cols_ref[...])
+    beta_out[...] = beta
+    set_terms(own_tgt, tgt_ref, beta, ROWS - 2)
+    plan_line(
+        patched(own_tgt, tgt_ref), tgt_ref.shape[1], patched(own_src, src_ref), src_ref.shape[1], line_ref
+    )
+    row_out[...] = jnp.broadcast_to((line_ref[...] - alpha_ref[...])[None], row_out.shape)
+
+
+def last_column_kernel(
+    share_count, rows_ref, src_ref, src_mass_ref, own_tgt, tgt_ref, beta_ref, col_out, merged_out, own_src, line_ref
+):
     merged = merge(rows_ref[...])
     merged_out[...] = merged
-    pieces = as_rows(column_line(merged, src_ref, src_mass_ref, tgt_ref, own_src))
-    share = len(pieces) // share_count
+    set_terms(own_src, src_ref, src_mass_ref[...] - merged, ROWS - 1)
+    plan_line(
+        patched(own_src, src_ref), src_ref.shape[1], patched(own_tgt, tgt_ref), tgt_ref.shape[1], line_ref
+    )
+    line = line_ref[...] - beta_ref[...]
+    share = line.shape[0] // share_count
     for part in range(share_count):
-        block = jnp.concatenate(pieces[part * share : part * share + share], axis=0)
         for to in range(part, col_out.shape[0], share_count):
-            col_out[to] = block
+            col_out[to] = line[part * share : part * share + share]
 
 
 def final_kernel(near, cols_ref, rows_ref, src_ref, tgt_ref, row_out, pot_out):
@@ -231,7 +272,7 @@
         for shift in range(1, share_count)
     ]
     src_all = swap(src_send, near)
-    row_send, src, tgt, src_mass, tgt_mass = call(
+    row_send, src, tgt, src_mass, tgt_mass, beta = call(
         functools.partial(first_kernel, dims, share_count),
         (
             shape(near_count, row_tiles, LANES),
@@ -239,24 +280,28 @@
             shape(depth, cols, dtype=BF16),
             shape(row_tiles, LANES),
             shape(col_tiles, LANES),
+            shape(col_tiles, LANES),
         ),
         [pltpu.VMEM((share_count, ROWS, own_cols), F32)],
     )(src_all, *tgts)
-    changed = 3 * ROWS
     row_all = swap(row_send, near)
-    col_send = call(
-        column_kernel, shape(far_count, col_tiles, LANES), [pltpu.VMEM((changed, rows), BF16)]
-    )(row_all, src, src_mass, tgt)
+    col_send, alpha, own_src = call(
+        column_kernel,
+        (shape(far_count, col_tiles, LANES), shape(row_tiles, LANES), shape(3 * ROWS, rows, dtype=BF16)),
+        [pltpu.VMEM((col_tiles, LANES), F32)],
+    )(row_all, src, src_mass, tgt, beta)
     col_all = swap(col_send, far)
-    row_send = call(
-        row_kernel, shape(near_count, row_tiles, LANES), [pltpu.VMEM((changed, cols), BF16)]
-    )(col_all, src, tgt, tgt_mass)
+    row_send, own_tgt, beta = call(
+        row_kernel,
+        (shape(near_count, row_tiles, LANES), shape(3 * ROWS, cols, dtype=BF16), shape(col_tiles, LANES)),
+        [pltpu.VMEM((row_tiles, LANES), F32)],
+    )(col_all, own_src, src, tgt, tgt_mass, alpha)
     row_all = swap(row_send, near)
     col_send, merged = call(
         functools.partial(last_column_kernel, share_count),
         (shape(far_count, own_cols // LANES, LANES), shape(row_tiles, LANES)),
-        [pltpu.VMEM((changed, rows), BF16)],
-    )(row_all, src, src_mass, tgt)
+        [pltpu.VMEM((3 * ROWS, rows), BF16), pltpu.VMEM((col_tiles, LANES), F32)],
+    )(row_all, src, src_mass, own_tgt, tgt, beta)
     col_all = swap(col_send, far)
     row_potential, column_potential = call(
         functools.partial(final_kernel, near), (shape(1, own_rows), shape(own_cols // LANES, LANES))

time: 76.3 us -> 77.2 us (1.012)
  Pallas kernels: 9.84 us -> 10.7 us
    pallas_call x2, Pallas kernels: 3.72 us -> 4.78 us  [the longest x1 3.28 us: on_device(): call(column_kernel, (shape(far_count, col_tiles, LANES), shape(row_tiles,...]
where the time goes in v4:
time: 77.2 us; the launch traced here: 76.7 us
  blocking collectives  50.2 us (65%)
  Pallas kernels  10.7 us (14%)
  starting transfers between devices  8.63 us (11%)
  waiting for transfers between devices  6.5 us (8%)
    all_to_all x4, blocking collectives, swap(): return lax.all_to_all(value, axes, 0, 0, tiled=True)  50.2 us
    all_to_all x1, starting transfers between devices, swap(): return lax.all_to_all(value, axes, 0, 0, tiled=True)  7.58 us
    all_to_all x1, waiting for transfers between devices, swap(): return lax.all_to_all(value, axes, 0, 0, tiled=True)  5.6 us
    pallas_call x1, Pallas kernels, on_device(): call(column_kernel, (shape(far_count, col_tiles, LANES), shape(row_tiles,...  3.28 us
    pallas_call x1, Pallas kernels, on_device(): call(functools.partial(first_kernel, dims, share_count), (shape(near_coun...  2.04 us
    pallas_call x1, Pallas kernels, on_device(): call(pack_kernel, (shape(near_count, ROWS, LANES), shape(ROWS, own_cols))...  1.66 us
    pallas_call x1, Pallas kernels, on_device(): call(functools.partial(last_column_kernel, share_count), (shape(far_count...  1.55 us
  transfers between devices with their start and end apart: 2, of which 2 were waited for; matrix products, arithmetic and copies ran while one was open for 0% of the time, Pallas kernels for 0%

profile of v4, /device:TPU:1, one launch (start us, length us, event | category | flops | bytes accessed | tf_op | source)
XLA Modules:
  0.0 76.7 jit_solution(2627245829216012001)
XLA Ops:
  0.6 1.7 %shard_map.68 = (f32[16,32,128]{2,1,0:T(8,128)}, f32[32,512]{1,0:T(8,128)S(1)}) custom-call(f32[30,128]{1,0:T(8,128)} %src_ref.1, f32[1,128]{1,0:T(1,128)} %bitcast.7, f32[30,512]{1,0:T(8,128)} %tgt_ref.1, f32[1,512]{1,0:T(1,128)} %bitcast.5, f32[1,512]{1,0:T(1,128)} %bitcast.6), custom_call_target="tpu_custom_call" | custom-call | tf_op jit(solution)/shard_map/pallas_call | solution.py:264
  2.3 7.6 %all-to-all-start = ((f32[16,32,128]{2,1,0:T(8,128)}), f32[16,32,128]{2,1,0:T(8,128)S(1)}, u32[]{:S(2)}, u32[]{:S(2)}) async-start(f32[16,32,128]{2,1,0:T(8,128)} %get-tuple-element.20), calls=%async_computation | async-start | bytes 524288 | tf_op jit(solution)/shard_map/all_to_all | solution.py:261
  9.9 1.0 %collective-permute-start = (f32[32,512]{1,0:T(8,128)S(1)}, f32[32,512]{1,0:T(8,128)S(1)}, u32[]{:S(2)}, u32[]{:S(2)}) collective-permute-start(f32[32,512]{1,0:T(8,128)S(1)} %get-tuple-element.21.refs_0_), channel_id=1, source_target_pairs={{0,1},{1,0},{2,3},{3,2},{4,5},{5,4},{6,7},{7,6},{8,9},{9,8},{10,11... | collective-permute-start | bytes 196616 | tf_op jit(solution)/shard_map/ppermute | solution.py:271
  10.9 0.9 %collective-permute-done.refs_1_ = f32[32,512]{1,0:T(8,128)S(1)} collective-permute-done((f32[32,512]{1,0:T(8,128)S(1)}, f32[32,512]{1,0:T(8,128)S(1)}, u32[]{:S(2)}, u32[]{:S(2)}) %collective-permute-start) | collective-permute-done | bytes 65568 | tf_op jit(solution)/shard_map/ppermute | solution.py:271
  11.8 5.6 %all-to-all-done.src_ref = f32[16,32,128]{2,1,0:T(8,128)S(1)} async-done(((f32[16,32,128]{2,1,0:T(8,128)}), f32[16,32,128]{2,1,0:T(8,128)S(1)}, u32[]{:S(2)}, u32[]{:S(2)}) %all-to-all-start) | async-done | bytes 262176 | tf_op jit(solution)/shard_map/all_to_all | solution.py:261
  17.4 2.0 %shard_map.69 = (f32[16,16,128]{2,1,0:T(8,128)S(1)}, bf16[192,2048]{1,0:T(8,128)(2,1)S(1)}, bf16[192,1024]{1,0:T(8,128)(2,1)S(1)}, f32[16,128]{1,0:T(8,128)S(1)}...) custom-call(f32[16,32,128]{2,1,0:T(8,128)S(1)} %all-to-all-done.src_ref, f32[32,512]{1,0:T(8,128)S(1)} %get-tuple-element.21.refs_0_, ...), custom_call_target="tpu_custom_call" | custom-call | tf_op jit(solution)/shard_map/pallas_call | solution.py:275
  19.5 9.8 %all_to_all.25.rows_ref = f32[16,16,128]{2,1,0:T(8,128)S(1)} all-to-all(f32[16,16,128]{2,1,0:T(8,128)S(1)} %get-tuple-element.22), channel_id=1, replica_groups=mesh['z'=8,'y'=4,'x'=4,'c'=2] {'y','x'}, dimensions={0} | all-to-all | bytes 262144 | tf_op jit(solution)/shard_map/all_to_all | solution.py:261
  29.2 3.3 %shard_map.70 = (f32[16,8,128]{2,1,0:T(8,128)S(1)}, f32[16,128]{1,0:T(8,128)S(1)}, bf16[96,2048]{1,0:T(8,128)(2,1)S(1)}) custom-call(f32[16,16,128]{2,1,0:T(8,128)S(1)} %all_to_all.25.rows_ref, bf16[192,2048]{1,0:T(8,128)(2,1)S(1)} %get-tuple-element.23.src_ref, f32[16,128]{1,0:T(8,128)S(1)} %get-tuple-element.24.src_mass_ref, ...), custom_call_target="tpu_custom_call" | custom-call | tf_op jit(solution)/shard_map/pallas_call | solution.py:288
  32.5 19.3 %all_to_all.26.cols_ref = f32[16,8,128]{2,1,0:T(8,128)S(1)} all-to-all(f32[16,8,128]{2,1,0:T(8,128)S(1)} %get-tuple-element.27), channel_id=1, replica_groups=mesh['z'=8,'y'=4,'x'=4,'c'=2] {'z','c'}, dimensions={0} | all-to-all | bytes 131072 | tf_op jit(solution)/shard_map/all_to_all | solution.py:261
  51.8 1.5 %shard_map.71 = (f32[16,16,128]{2,1,0:T(8,128)S(1)}, bf16[96,1024]{1,0:T(8,128)(2,1)S(1)}, f32[8,128]{1,0:T(8,128)S(1)}) custom-call(f32[16,8,128]{2,1,0:T(8,128)S(1)} %all_to_all.26.cols_ref, bf16[96,2048]{1,0:T(8,128)(2,1)S(1)} %get-tuple-element.28.own_src, bf16[192,2048]{1,0:T(8,128)(2,1)S(1)} %get-tuple-element.23.src_ref, ...), custom_call_target="tpu_custom_call" | custom-call | tf_op jit(solution)/shard_map/pallas_call | solution.py:294
  53.3 9.6 %all_to_all.27.rows_ref = f32[16,16,128]{2,1,0:T(8,128)S(1)} all-to-all(f32[16,16,128]{2,1,0:T(8,128)S(1)} %get-tuple-element.31), channel_id=1, replica_groups=mesh['z'=8,'y'=4,'x'=4,'c'=2] {'y','x'}, dimensions={0} | all-to-all | bytes 262144 | tf_op jit(solution)/shard_map/all_to_all | solution.py:261
  63.0 0.0 copy-start.1
  63.0 1.5 %shard_map.72 = (f32[16,4,128]{2,1,0:T(4,128)S(1)}, f32[16,128]{1,0:T(8,128)S(1)}) custom-call(f32[16,16,128]{2,1,0:T(8,128)S(1)} %all_to_all.27.rows_ref, bf16[192,2048]{1,0:T(8,128)(2,1)S(1)} %get-tuple-element.23.src_ref, f32[16,128]{1,0:T(8,128)S(1)} %get-tuple-element.24.src_mass_ref, bf16[96,1024]{1,0:T(8,128)(2,1)S(1)} %get-tuple-element.32.own_tgt, ...), custom_call_target="tpu_custom_call" | custom-call | tf_op jit(solution)/shard_map/pallas_call | solution.py:300
  64.5 0.0 copy-start
  64.5 11.6 %all_to_all.28.cols_ref = f32[16,4,128]{2,1,0:T(4,128)S(1)} all-to-all(f32[16,4,128]{2,1,0:T(4,128)S(1)} %get-tuple-element.34), channel_id=1, replica_groups=mesh['z'=8,'y'=4,'x'=4,'c'=2] {'z','c'}, dimensions={0} | all-to-all | bytes 65536 | tf_op jit(solution)/shard_map/all_to_all | solution.py:261
  76.1 0.0 copy-done.1
  76.1 0.0 copy-done
  76.1 0.6 shard_map.73
Async XLA Ops:
  2.3 15.1 %all-to-all-start = ((f32[16,32,128]{2,1,0:T(8,128)}), f32[16,32,128]{2,1,0:T(8,128)S(1)}, u32[]{:S(2)}, u32[]{:S(2)}) async-start(f32[16,32,128]{2,1,0:T(8,128)} %get-tuple-element.20), calls=%async_computation | async-start | bytes 524288 | tf_op jit(solution)/shard_map/all_to_all | solution.py:261
  9.9 1.9 %collective-permute-start = (f32[32,512]{1,0:T(8,128)S(1)}, f32[32,512]{1,0:T(8,128)S(1)}, u32[]{:S(2)}, u32[]{:S(2)}) collective-permute-start(f32[32,512]{1,0:T(8,128)S(1)} %get-tuple-element.21.refs_0_), channel_id=1, source_target_pairs={{0,1},{1,0},{2,3},{3,2},{4,5},{5,4},{6,7},{7,6},{8,9},{9,8},{10,11... | collective-permute-start | bytes 196616 | tf_op jit(solution)/shard_map/ppermute | solution.py:271
  63.0 13.1 %copy-start.1 = (f32[30,128]{1,0:T(8,128)S(1)}, f32[30,128]{1,0:T(8,128)}, u32[]{:S(2)}) copy-start(f32[30,128]{1,0:T(8,128)} %src_ref.1) | copy-start | bytes 46084
  64.5 11.6 %copy-start = (f32[30,512]{1,0:T(8,128)S(1)}, f32[30,512]{1,0:T(8,128)}, u32[]{:S(2)}) copy-start(f32[30,512]{1,0:T(8,128)} %tgt_ref.1) | copy-start | bytes 184324

commit v5 on v4

--- a/solution.py
+++ b/solution.py
@@ -113,11 +113,6 @@
         ref[row + at : row + at + 1, :] = piece
 
 
-def send_to_all(line, out_ref):
-    for at, piece in enumerate(as_rows(line)):
-        out_ref[:, at, :] = jnp.broadcast_to(piece, (out_ref.shape[0], LANES))
-
-
 def pack_kernel(*refs):
     inputs, (src_out, tgt_out), held, sems = refs[:5], refs[5:7], refs[7:12], refs[12]
     copies = [
@@ -134,26 +129,14 @@
     src_out[...] = jnp.broadcast_to(block[None], src_out.shape)
 
 
-def first_kernel(dims, share_count, src_ref, *refs):
+def target_kernel(dims, share_count, *refs):
     tgt_refs = refs[:share_count]
-    row_out, src_out, tgt_out, src_mass_out, tgt_mass_out, beta_out = refs[share_count : share_count + 6]
-    held = refs[share_count + 6]
+    tgt_out, tgt_mass_out, beta_out, top_out, held = refs[share_count:]
     mine = lax.axis_index("c")
     for shift in range(share_count):
         held[lax.rem(mine + share_count - shift, share_count)] = tgt_refs[shift][...]
-    groups = src_ref.shape[0]
-    for group in range(groups):
-        block = src_ref[group]
-        src_mass_out[group : group + 1, :] = LOG2E * block[dims : dims + 1, :]
-        spare = lax.broadcasted_iota(jnp.int32, block.shape, 0) >= dims
-        split = parts_of(jnp.where(spare, 0.0, (0.5 * LOG2E) * block))
-        lanes = slice(group * LANES, group * LANES + LANES)
-        for slot, which in enumerate(LEFT):
-            piece = split[which].astype(F32)
-            if slot < 3:
-                piece = with_row(piece, ROWS - 2, 1.0)
-            src_out[slot * ROWS : slot * ROWS + ROWS, lanes] = piece.astype(BF16)
     width = held.shape[2]
+    top = None
     for group in range(share_count):
         block = held[group]
         mass = LOG2E * block[dims : dims + 1, :]
@@ -162,7 +145,10 @@
         coords = jnp.where(spare, 0.0, block)
         split = parts_of(coords)
         norm = jnp.sum(coords * coords, axis=0, keepdims=True)
-        beta = mass + LOG2E * (0.5 * block[dims + 1 : dims + 2, :] - 0.25 * norm)
+        term = mass + (0.5 * LOG2E) * block[dims + 1 : dims + 2, :]
+        highest = jnp.max(term, axis=1, keepdims=True)
+        top = highest if top is None else jnp.maximum(top, highest)
+        beta = term - (0.25 * LOG2E) * norm
         set_rows(beta_out, beta, group * (width // LANES))
         beta_parts = parts_of(beta)
         lanes = slice(group * width, group * width + width)
@@ -172,7 +158,28 @@
                 piece = with_row(piece, ROWS - 2, beta_parts[slot].astype(F32))
                 piece = with_row(piece, ROWS - 1, 1.0)
             tgt_out[slot * ROWS : slot * ROWS + ROWS, lanes] = piece.astype(BF16)
-    send_to_all(fold(whole(tgt_out), tgt_out.shape[1], whole(src_out), src_out.shape[1]), row_out)
+    top_out[...] = jnp.broadcast_to(top, top_out.shape)
+
+
+def first_kernel(dims, src_ref, tgt_ref, top_ref, row_out, src_out, src_mass_out, alpha_ref, line_ref):
+    for group in range(src_ref.shape[0]):
+        block = src_ref[group]
+        src_mass_out[group : group + 1, :] = LOG2E * block[dims : dims + 1, :]
+        spare = lax.broadcasted_iota(jnp.int32, block.shape, 0) >= dims
+        coords = jnp.where(spare, 0.0, block)
+        split = parts_of((0.5 * LOG2E) * coords)
+        alpha = (-0.25 * LOG2E) * jnp.sum(coords * coords, axis=0, keepdims=True) - top_ref[...]
+        alpha_ref[group : group + 1, :] = alpha
+        alpha_parts = parts_of(alpha)
+        lanes = slice(group * LANES, group * LANES + LANES)
+        for slot, which in enumerate(LEFT):
+            piece = split[which].astype(F32)
+            if slot < 3:
+                piece = with_row(piece, ROWS - 2, 1.0)
+                piece = with_row(piece, ROWS - 1, alpha_parts[slot].astype(F32))
+            src_out[slot * ROWS : slot * ROWS + ROWS, lanes] = piece.astype(BF16)
+    plan_line(whole(tgt_ref), tgt_ref.shape[1], whole(src_out), src_out.shape[1], line_ref)
+    row_out[...] = jnp.broadcast_to((line_ref[...] - alpha_ref[...])[None], row_out.shape)
 
 
 def set_terms(own_ref, ref, values, row):
@@ -272,18 +279,25 @@
         for shift in range(1, share_count)
     ]
     src_all = swap(src_send, near)
-    row_send, src, tgt, src_mass, tgt_mass, beta = call(
-        functools.partial(first_kernel, dims, share_count),
+    tgt, tgt_mass, beta, top = call(
+        functools.partial(target_kernel, dims, share_count),
+        (
+            shape(depth, cols, dtype=BF16),
+            shape(col_tiles, LANES),
+            shape(col_tiles, LANES),
+            shape(1, LANES),
+        ),
+        [pltpu.VMEM((share_count, ROWS, own_cols), F32)],
+    )(*tgts)
+    row_send, src, src_mass = call(
+        functools.partial(first_kernel, dims),
         (
             shape(near_count, row_tiles, LANES),
             shape(depth, rows, dtype=BF16),
-            shape(depth, cols, dtype=BF16),
             shape(row_tiles, LANES),
-            shape(col_tiles, LANES),
-            shape(col_tiles, LANES),
         ),
-        [pltpu.VMEM((share_count, ROWS, own_cols), F32)],
-    )(src_all, *tgts)
+        [pltpu.VMEM((row_tiles, LANES), F32)] * 2,
+    )(src_all, tgt, top)
     row_all = swap(row_send, near)
     col_send, alpha, own_src = call(
         column_kernel,

time: 77.2 us -> 78.4 us (1.016)
  Pallas kernels: 10.7 us -> 12 us
    pallas_call x1 -> x2, Pallas kernels: 2.04 us -> 3.41 us  [the longest x1 3.31 us: on_device(): call(functools.partial(first_kernel, dims), (shape(near_count, row_tiles,...]
where the time goes in v5:
time: 78.4 us; the launch traced here: 78 us
  blocking collectives  50.2 us (64%)
  Pallas kernels  12 us (15%)
  starting transfers between devices  8.63 us (11%)
  waiting for transfers between devices  6.39 us (8%)
    all_to_all x4, blocking collectives, swap(): return lax.all_to_all(value, axes, 0, 0, tiled=True)  50.2 us
    all_to_all x1, starting transfers between devices, swap(): return lax.all_to_all(value, axes, 0, 0, tiled=True)  7.58 us
    all_to_all x1, waiting for transfers between devices, swap(): return lax.all_to_all(value, axes, 0, 0, tiled=True)  5.49 us
    pallas_call x1, Pallas kernels, on_device(): call(functools.partial(first_kernel, dims), (shape(near_count, row_tiles,...  3.31 us
    pallas_call x1, Pallas kernels, on_device(): call(column_kernel, (shape(far_count, col_tiles, LANES), shape(row_tiles,...  3.28 us
    pallas_call x1, Pallas kernels, on_device(): call(pack_kernel, (shape(near_count, ROWS, LANES), shape(ROWS, own_cols))...  1.66 us
  transfers between devices with their start and end apart: 2, of which 2 were waited for; matrix products, arithmetic and copies ran while one was open for 0% of the time, Pallas kernels for 0%

profile of v5, /device:TPU:1, one launch (start us, length us, event | category | flops | bytes accessed | tf_op | source)
XLA Modules:
  0.0 78.0 jit_solution(13333650058079387390)
XLA Ops:
  0.6 1.7 %shard_map.68 = (f32[16,32,128]{2,1,0:T(8,128)}, f32[32,512]{1,0:T(8,128)S(1)}) custom-call(f32[30,128]{1,0:T(8,128)} %src_ref.1, f32[1,128]{1,0:T(1,128)} %bitcast.7, f32[30,512]{1,0:T(8,128)} %tgt_ref.1, f32[1,512]{1,0:T(1,128)} %bitcast.5, f32[1,512]{1,0:T(1,128)} %bitcast.6), custom_call_target="tpu_custom_call" | custom-call | tf_op jit(solution)/shard_map/pallas_call | solution.py:271
  2.3 7.6 %all-to-all-start = ((f32[16,32,128]{2,1,0:T(8,128)}), f32[16,32,128]{2,1,0:T(8,128)S(1)}, u32[]{:S(2)}, u32[]{:S(2)}) async-start(f32[16,32,128]{2,1,0:T(8,128)} %get-tuple-element.21), calls=%async_computation | async-start | bytes 524288 | tf_op jit(solution)/shard_map/all_to_all | solution.py:268
  9.9 1.0 %collective-permute-start = (f32[32,512]{1,0:T(8,128)S(1)}, f32[32,512]{1,0:T(8,128)S(1)}, u32[]{:S(2)}, u32[]{:S(2)}) collective-permute-start(f32[32,512]{1,0:T(8,128)S(1)} %get-tuple-element.22.refs_0_), channel_id=1, source_target_pairs={{0,1},{1,0},{2,3},{3,2},{4,5},{5,4},{6,7},{7,6},{8,9},{9,8},{10,11... | collective-permute-start | bytes 196616 | tf_op jit(solution)/shard_map/ppermute | solution.py:278
  10.9 0.9 %collective-permute-done.refs_1_ = f32[32,512]{1,0:T(8,128)S(1)} collective-permute-done((f32[32,512]{1,0:T(8,128)S(1)}, f32[32,512]{1,0:T(8,128)S(1)}, u32[]{:S(2)}, u32[]{:S(2)}) %collective-permute-start) | collective-permute-done | bytes 65568 | tf_op jit(solution)/shard_map/ppermute | solution.py:278
  11.8 0.1 shard_map.69
  11.9 5.5 %all-to-all-done.src_ref = f32[16,32,128]{2,1,0:T(8,128)S(1)} async-done(((f32[16,32,128]{2,1,0:T(8,128)}), f32[16,32,128]{2,1,0:T(8,128)S(1)}, u32[]{:S(2)}, u32[]{:S(2)}) %all-to-all-start) | async-done | bytes 262176 | tf_op jit(solution)/shard_map/all_to_all | solution.py:268
  17.4 3.3 %shard_map.70 = (f32[16,16,128]{2,1,0:T(8,128)S(1)}, bf16[192,2048]{1,0:T(8,128)(2,1)S(1)}, f32[16,128]{1,0:T(8,128)S(1)}) custom-call(f32[16,32,128]{2,1,0:T(8,128)S(1)} %all-to-all-done.src_ref, bf16[192,1024]{1,0:T(8,128)(2,1)S(1)} %get-tuple-element.23.tgt_ref, f32[1,128]{1,0:T(1,128)S(1)} %get-tuple-element.24.top_ref), custom_call_target="tpu_custom_call" | custom-call | tf_op jit(solution)/shard_map/pallas_call | solution.py:292
  20.7 9.8 %all_to_all.25.rows_ref = f32[16,16,128]{2,1,0:T(8,128)S(1)} all-to-all(f32[16,16,128]{2,1,0:T(8,128)S(1)} %get-tuple-element.25), channel_id=1, replica_groups=mesh['z'=8,'y'=4,'x'=4,'c'=2] {'y','x'}, dimensions={0} | all-to-all | bytes 262144 | tf_op jit(solution)/shard_map/all_to_all | solution.py:268
  30.5 3.3 %shard_map.71 = (f32[16,8,128]{2,1,0:T(8,128)S(1)}, f32[16,128]{1,0:T(8,128)S(1)}, bf16[96,2048]{1,0:T(8,128)(2,1)S(1)}) custom-call(f32[16,16,128]{2,1,0:T(8,128)S(1)} %all_to_all.25.rows_ref, bf16[192,2048]{1,0:T(8,128)(2,1)S(1)} %get-tuple-element.26.src_ref, f32[16,128]{1,0:T(8,128)S(1)} %get-tuple-element.27.src_mass_ref, ...), custom_call_target="tpu_custom_call" | custom-call | tf_op jit(solution)/shard_map/pallas_call | solution.py:302
  33.8 19.3 %all_to_all.26.cols_ref = f32[16,8,128]{2,1,0:T(8,128)S(1)} all-to-all(f32[16,8,128]{2,1,0:T(8,128)S(1)} %get-tuple-element.29), channel_id=1, replica_groups=mesh['z'=8,'y'=4,'x'=4,'c'=2] {'z','c'}, dimensions={0} | all-to-all | bytes 131072 | tf_op jit(solution)/shard_map/all_to_all | solution.py:268
  53.1 1.5 %shard_map.72 = (f32[16,16,128]{2,1,0:T(8,128)S(1)}, bf16[96,1024]{1,0:T(8,128)(2,1)S(1)}, f32[8,128]{1,0:T(8,128)S(1)}) custom-call(f32[16,8,128]{2,1,0:T(8,128)S(1)} %all_to_all.26.cols_ref, bf16[96,2048]{1,0:T(8,128)(2,1)S(1)} %get-tuple-element.30.own_src, bf16[192,2048]{1,0:T(8,128)(2,1)S(1)} %get-tuple-element.26.src_ref, ...), custom_call_target="tpu_custom_call" | custom-call | tf_op jit(solution)/shard_map/pallas_call | solution.py:308
  54.6 9.6 %all_to_all.27.rows_ref = f32[16,16,128]{2,1,0:T(8,128)S(1)} all-to-all(f32[16,16,128]{2,1,0:T(8,128)S(1)} %get-tuple-element.33), channel_id=1, replica_groups=mesh['z'=8,'y'=4,'x'=4,'c'=2] {'y','x'}, dimensions={0} | all-to-all | bytes 262144 | tf_op jit(solution)/shard_map/all_to_all | solution.py:268
  64.2 0.0 copy-start.1
  64.2 1.5 %shard_map.73 = (f32[16,4,128]{2,1,0:T(4,128)S(1)}, f32[16,128]{1,0:T(8,128)S(1)}) custom-call(f32[16,16,128]{2,1,0:T(8,128)S(1)} %all_to_all.27.rows_ref, bf16[192,2048]{1,0:T(8,128)(2,1)S(1)} %get-tuple-element.26.src_ref, f32[16,128]{1,0:T(8,128)S(1)} %get-tuple-element.27.src_mass_ref, bf16[96,1024]{1,0:T(8,128)(2,1)S(1)} %get-tuple-element.34.own_tgt, ...), custom_call_target="tpu_custom_call" | custom-call | tf_op jit(solution)/shard_map/pallas_call | solution.py:314
  65.8 0.0 copy-start
  65.8 11.5 %all_to_all.28.cols_ref = f32[16,4,128]{2,1,0:T(4,128)S(1)} all-to-all(f32[16,4,128]{2,1,0:T(4,128)S(1)} %get-tuple-element.36), channel_id=1, replica_groups=mesh['z'=8,'y'=4,'x'=4,'c'=2] {'z','c'}, dimensions={0} | all-to-all | bytes 65536 | tf_op jit(solution)/shard_map/all_to_all | solution.py:268
  77.3 0.0 copy-done.1
  77.3 0.0 copy-done
  77.3 0.6 shard_map.74
Async XLA Ops:
  2.3 15.1 %all-to-all-start = ((f32[16,32,128]{2,1,0:T(8,128)}), f32[16,32,128]{2,1,0:T(8,128)S(1)}, u32[]{:S(2)}, u32[]{:S(2)}) async-start(f32[16,32,128]{2,1,0:T(8,128)} %get-tuple-element.21), calls=%async_computation | async-start | bytes 524288 | tf_op jit(solution)/shard_map/all_to_all | solution.py:268
  9.9 1.9 %collective-permute-start = (f32[32,512]{1,0:T(8,128)S(1)}, f32[32,512]{1,0:T(8,128)S(1)}, u32[]{:S(2)}, u32[]{:S(2)}) collective-permute-start(f32[32,512]{1,0:T(8,128)S(1)} %get-tuple-element.22.refs_0_), channel_id=1, source_target_pairs={{0,1},{1,0},{2,3},{3,2},{4,5},{5,4},{6,7},{7,6},{8,9},{9,8},{10,11... | collective-permute-start | bytes 196616 | tf_op jit(solution)/shard_map/ppermute | solution.py:278
  64.2 13.1 %copy-start.1 = (f32[30,128]{1,0:T(8,128)S(1)}, f32[30,128]{1,0:T(8,128)}, u32[]{:S(2)}) copy-start(f32[30,128]{1,0:T(8,128)} %src_ref.1) | copy-start | bytes 46084
  65.8 11.6 %copy-start = (f32[30,512]{1,0:T(8,128)S(1)}, f32[30,512]{1,0:T(8,128)}, u32[]{:S(2)}) copy-start(f32[30,512]{1,0:T(8,128)} %tgt_ref.1) | copy-start | bytes 184324

commit v6 on v5

--- a/solution.py
+++ b/solution.py
@@ -113,8 +113,9 @@
         ref[row + at : row + at + 1, :] = piece
 
 
-def pack_kernel(*refs):
-    inputs, (src_out, tgt_out), held, sems = refs[:5], refs[5:7], refs[7:12], refs[12]
+def pack_kernel(copies_out, spare_rows, *refs):
+    count = len(refs) // 2 - 1
+    inputs, out, held, sems = refs[:count], refs[count], refs[count + 1 : -1], refs[-1]
     copies = [
         pltpu.make_async_copy(whence, where, sems.at[at])
         for at, (whence, where) in enumerate(zip(inputs, held))
@@ -123,10 +124,22 @@
         copy.start()
     for copy in copies:
         copy.wait()
-    src, src_mass, tgt, tgt_mass, start = (ref[...] for ref in held)
-    tgt_out[...] = jnp.concatenate([tgt, tgt_mass, start], axis=0)
-    block = jnp.concatenate([src, src_mass, jnp.zeros((1, LANES), F32)], axis=0)
-    src_out[...] = jnp.broadcast_to(block[None], src_out.shape)
+    rows = [ref[...] for ref in held]
+    if spare_rows:
+        rows.append(jnp.zeros((spare_rows, rows[0].shape[1]), F32))
+    block = jnp.concatenate(rows, axis=0)
+    out[...] = jnp.broadcast_to(block[None], out.shape) if copies_out else block
+
+
+def pack(given, out):
+    copies_out = len(out.shape) == 3
+    spare_rows = ROWS - sum(array.shape[0] for array in given)
+    return call(
+        functools.partial(pack_kernel, copies_out, spare_rows),
+        out,
+        [pltpu.VMEM(array.shape, F32) for array in given] + [pltpu.SemaphoreType.DMA((len(given),))],
+        in_specs=[pl.BlockSpec(memory_space=pl.ANY)] * len(given),
+    )(*[pltpu.with_memory_space_constraint(array, pltpu.HBM) for array in given])
 
 
 def target_kernel(dims, share_count, *refs):
@@ -267,18 +280,13 @@
     def swap(value, axes):
         return lax.all_to_all(value, axes, 0, 0, tiled=True)
 
-    given = (sources, log_source_mass[None], targets, log_target_mass[None], start_potential[None])
-    src_send, tgt_own = call(
-        pack_kernel,
-        (shape(near_count, ROWS, LANES), shape(ROWS, own_cols)),
-        [pltpu.VMEM(array.shape, F32) for array in given] + [pltpu.SemaphoreType.DMA((len(given),))],
-        in_specs=[pl.BlockSpec(memory_space=pl.ANY)] * len(given),
-    )(*[pltpu.with_memory_space_constraint(array, pltpu.HBM) for array in given])
+    src_send = pack((sources, log_source_mass[None]), shape(near_count, ROWS, LANES))
+    src_all = swap(src_send, near)
+    tgt_own = pack((targets, log_target_mass[None], start_potential[None]), shape(ROWS, own_cols))
     tgts = [tgt_own] + [
         lax.ppermute(tgt_own, "c", [(k, (k + shift) % share_count) for k in range(share_count)])
         for shift in range(1, share_count)
     ]
-    src_all = swap(src_send, near)
     tgt, tgt_mass, beta, top = call(
         functools.partial(target_kernel, dims, share_count),
         (

time: 78.4 us -> 78.2 us (level)
  waiting for transfers between devices: 6.39 us -> 5.51 us
    all_to_all x1, waiting for transfers between devices: 5.49 us -> 4.6 us  [swap(): return lax.all_to_all(value, axes, 0, 0, tiled=True)]
    pallas_call x1 -> x2, Pallas kernels: 1.66 us -> 2.35 us  [pack(): call(functools.partial(pack_kernel, copies_out, spare_rows), out, [pltpu....]
  transfers between devices with their start and end apart: 2 -> 2, of which waited for: 2 -> 2; matrix products, arithmetic and copies ran while one was open for 0% -> 0% of each run, Pallas kernels for 0% -> 1%
where the time goes in v6:
time: 78.2 us; the launch traced here: 77.8 us
  blocking collectives  50.2 us (64%)
  Pallas kernels  12.7 us (16%)
  starting transfers between devices  8.63 us (11%)
  waiting for transfers between devices  5.51 us (7%)
    all_to_all x4, blocking collectives, swap(): return lax.all_to_all(value, axes, 0, 0, tiled=True)  50.2 us
    all_to_all x1, starting transfers between devices, swap(): return lax.all_to_all(value, axes, 0, 0, tiled=True)  7.58 us
    all_to_all x1, waiting for transfers between devices, swap(): return lax.all_to_all(value, axes, 0, 0, tiled=True)  4.6 us
    pallas_call x1, Pallas kernels, on_device(): call(functools.partial(first_kernel, dims), (shape(near_count, row_tiles,...  3.31 us
    pallas_call x1, Pallas kernels, on_device(): call(column_kernel, (shape(far_count, col_tiles, LANES), shape(row_tiles,...  3.28 us
    pallas_call x2, Pallas kernels, pack(): call(functools.partial(pack_kernel, copies_out, spare_rows), out, [pltpu....  2.35 us
  transfers between devices with their start and end apart: 2, of which 2 were waited for; matrix products, arithmetic and copies ran while one was open for 0% of the time, Pallas kernels for 1%

profile of v6, /device:TPU:1, one launch (start us, length us, event | category | flops | bytes accessed | tf_op | source)
XLA Modules:
  0.0 77.8 jit_solution(15019405860516961173)
XLA Ops:
  0.6 1.5 %shard_map.68 = f32[16,32,128]{2,1,0:T(8,128)} custom-call(f32[30,128]{1,0:T(8,128)} %src_ref.1, f32[1,128]{1,0:T(1,128)} %bitcast.7), custom_call_target="tpu_custom_call" | custom-call | tf_op jit(solution)/shard_map/pallas_call | solution.py:137
  2.1 7.6 %all-to-all-start = ((f32[16,32,128]{2,1,0:T(8,128)}), f32[16,32,128]{2,1,0:T(8,128)S(1)}, u32[]{:S(2)}, u32[]{:S(2)}) async-start(f32[16,32,128]{2,1,0:T(8,128)} %shard_map.68), calls=%async_computation | async-start | bytes 524288 | tf_op jit(solution)/shard_map/all_to_all | solution.py:281
  9.7 0.9 %shard_map.69.refs_0_ = f32[32,512]{1,0:T(8,128)S(1)} custom-call(f32[30,512]{1,0:T(8,128)} %tgt_ref.1, f32[1,512]{1,0:T(1,128)} %bitcast.5, f32[1,512]{1,0:T(1,128)} %bitcast.6), custom_call_target="tpu_custom_call" | custom-call | tf_op jit(solution)/shard_map/pallas_call | solution.py:137
  10.6 1.0 %collective-permute-start = (f32[32,512]{1,0:T(8,128)S(1)}, f32[32,512]{1,0:T(8,128)S(1)}, u32[]{:S(2)}, u32[]{:S(2)}) collective-permute-start(f32[32,512]{1,0:T(8,128)S(1)} %shard_map.69.refs_0_), channel_id=1, source_target_pairs={{0,1},{1,0},{2,3},{3,2},{4,5},{5,4},{6,7},{7,6},{8,9},{9,8},{10,11... | collective-permute-start | bytes 196616 | tf_op jit(solution)/shard_map/ppermute | solution.py:287
  11.6 0.9 %collective-permute-done.refs_1_ = f32[32,512]{1,0:T(8,128)S(1)} collective-permute-done((f32[32,512]{1,0:T(8,128)S(1)}, f32[32,512]{1,0:T(8,128)S(1)}, u32[]{:S(2)}, u32[]{:S(2)}) %collective-permute-start) | collective-permute-done | bytes 65568 | tf_op jit(solution)/shard_map/ppermute | solution.py:287
  12.5 0.1 shard_map.70
  12.6 4.6 %all-to-all-done.src_ref = f32[16,32,128]{2,1,0:T(8,128)S(1)} async-done(((f32[16,32,128]{2,1,0:T(8,128)}), f32[16,32,128]{2,1,0:T(8,128)S(1)}, u32[]{:S(2)}, u32[]{:S(2)}) %all-to-all-start) | async-done | bytes 262176 | tf_op jit(solution)/shard_map/all_to_all | solution.py:281
  17.2 3.3 %shard_map.71 = (f32[16,16,128]{2,1,0:T(8,128)S(1)}, bf16[192,2048]{1,0:T(8,128)(2,1)S(1)}, f32[16,128]{1,0:T(8,128)S(1)}) custom-call(f32[16,32,128]{2,1,0:T(8,128)S(1)} %all-to-all-done.src_ref, bf16[192,1024]{1,0:T(8,128)(2,1)S(1)} %get-tuple-element.19.tgt_ref, f32[1,128]{1,0:T(1,128)S(1)} %get-tuple-element.20.top_ref), custom_call_target="tpu_custom_call" | custom-call | tf_op jit(solution)/shard_map/pallas_call | solution.py:300
  20.6 9.8 %all_to_all.25.rows_ref = f32[16,16,128]{2,1,0:T(8,128)S(1)} all-to-all(f32[16,16,128]{2,1,0:T(8,128)S(1)} %get-tuple-element.21), channel_id=1, replica_groups=mesh['z'=8,'y'=4,'x'=4,'c'=2] {'y','x'}, dimensions={0} | all-to-all | bytes 262144 | tf_op jit(solution)/shard_map/all_to_all | solution.py:281
  30.3 3.3 %shard_map.72 = (f32[16,8,128]{2,1,0:T(8,128)S(1)}, f32[16,128]{1,0:T(8,128)S(1)}, bf16[96,2048]{1,0:T(8,128)(2,1)S(1)}) custom-call(f32[16,16,128]{2,1,0:T(8,128)S(1)} %all_to_all.25.rows_ref, bf16[192,2048]{1,0:T(8,128)(2,1)S(1)} %get-tuple-element.22.src_ref, f32[16,128]{1,0:T(8,128)S(1)} %get-tuple-element.23.src_mass_ref, ...), custom_call_target="tpu_custom_call" | custom-call | tf_op jit(solution)/shard_map/pallas_call | solution.py:310
  33.6 19.3 %all_to_all.26.cols_ref = f32[16,8,128]{2,1,0:T(8,128)S(1)} all-to-all(f32[16,8,128]{2,1,0:T(8,128)S(1)} %get-tuple-element.25), channel_id=1, replica_groups=mesh['z'=8,'y'=4,'x'=4,'c'=2] {'z','c'}, dimensions={0} | all-to-all | bytes 131072 | tf_op jit(solution)/shard_map/all_to_all | solution.py:281
  52.9 1.5 %shard_map.73 = (f32[16,16,128]{2,1,0:T(8,128)S(1)}, bf16[96,1024]{1,0:T(8,128)(2,1)S(1)}, f32[8,128]{1,0:T(8,128)S(1)}) custom-call(f32[16,8,128]{2,1,0:T(8,128)S(1)} %all_to_all.26.cols_ref, bf16[96,2048]{1,0:T(8,128)(2,1)S(1)} %get-tuple-element.26.own_src, bf16[192,2048]{1,0:T(8,128)(2,1)S(1)} %get-tuple-element.22.src_ref, ...), custom_call_target="tpu_custom_call" | custom-call | tf_op jit(solution)/shard_map/pallas_call | solution.py:316
  54.4 9.6 %all_to_all.27.rows_ref = f32[16,16,128]{2,1,0:T(8,128)S(1)} all-to-all(f32[16,16,128]{2,1,0:T(8,128)S(1)} %get-tuple-element.29), channel_id=1, replica_groups=mesh['z'=8,'y'=4,'x'=4,'c'=2] {'y','x'}, dimensions={0} | all-to-all | bytes 262144 | tf_op jit(solution)/shard_map/all_to_all | solution.py:281
  64.0 0.0 copy-start.1
  64.0 1.5 %shard_map.74 = (f32[16,4,128]{2,1,0:T(4,128)S(1)}, f32[16,128]{1,0:T(8,128)S(1)}) custom-call(f32[16,16,128]{2,1,0:T(8,128)S(1)} %all_to_all.27.rows_ref, bf16[192,2048]{1,0:T(8,128)(2,1)S(1)} %get-tuple-element.22.src_ref, f32[16,128]{1,0:T(8,128)S(1)} %get-tuple-element.23.src_mass_ref, bf16[96,1024]{1,0:T(8,128)(2,1)S(1)} %get-tuple-element.30.own_tgt, ...), custom_call_target="tpu_custom_call" | custom-call | tf_op jit(solution)/shard_map/pallas_call | solution.py:322
  65.6 0.0 copy-start
  65.6 11.5 %all_to_all.28.cols_ref = f32[16,4,128]{2,1,0:T(4,128)S(1)} all-to-all(f32[16,4,128]{2,1,0:T(4,128)S(1)} %get-tuple-element.32), channel_id=1, replica_groups=mesh['z'=8,'y'=4,'x'=4,'c'=2] {'z','c'}, dimensions={0} | all-to-all | bytes 65536 | tf_op jit(solution)/shard_map/all_to_all | solution.py:281
  77.1 0.0 copy-done.1
  77.1 0.0 copy-done
  77.1 0.6 shard_map.75
Async XLA Ops:
  2.1 15.1 %all-to-all-start = ((f32[16,32,128]{2,1,0:T(8,128)}), f32[16,32,128]{2,1,0:T(8,128)S(1)}, u32[]{:S(2)}, u32[]{:S(2)}) async-start(f32[16,32,128]{2,1,0:T(8,128)} %shard_map.68), calls=%async_computation | async-start | bytes 524288 | tf_op jit(solution)/shard_map/all_to_all | solution.py:281
  10.6 1.9 %collective-permute-start = (f32[32,512]{1,0:T(8,128)S(1)}, f32[32,512]{1,0:T(8,128)S(1)}, u32[]{:S(2)}, u32[]{:S(2)}) collective-permute-start(f32[32,512]{1,0:T(8,128)S(1)} %shard_map.69.refs_0_), channel_id=1, source_target_pairs={{0,1},{1,0},{2,3},{3,2},{4,5},{5,4},{6,7},{7,6},{8,9},{9,8},{10,11... | collective-permute-start | bytes 196616 | tf_op jit(solution)/shard_map/ppermute | solution.py:287
  64.0 13.1 %copy-start.1 = (f32[30,128]{1,0:T(8,128)S(1)}, f32[30,128]{1,0:T(8,128)}, u32[]{:S(2)}) copy-start(f32[30,128]{1,0:T(8,128)} %src_ref.1) | copy-start | bytes 46084
  65.6 11.6 %copy-start = (f32[30,512]{1,0:T(8,128)S(1)}, f32[30,512]{1,0:T(8,128)}, u32[]{:S(2)}) copy-start(f32[30,512]{1,0:T(8,128)} %tgt_ref.1) | copy-start | bytes 184324
